TPU v7x, 32 devices: a whole 2x2x4 slice. The times are simulated.
32 devices in a mesh: blk: 8 (over z, x), head: 4 (over y, core).
Axes of the slice: x: 2, y: 2, z: 4, core: 2. Of those that a mesh axis runs over, the one named last changes fastest.
Arguments:
- tokens: bfloat16 [16384, 1536], P(('blk', 'head')), may hold values from -6 to 6
- segment: int32 [16384], P('blk'), may hold values from 0 to 15, never falling along the last dimension, each value on 1 to 2000 neighbouring positions
- norm1_gain: float32 [1536], P(('blk', 'head')), may hold values from 0.5 to 1.5
- w_query: float32 [1536, 1536], P(('blk', 'head')), may hold values from -0.15625 to 0.15625
- w_key: float32 [1536, 1536], P(('blk', 'head')), may hold values from -0.15625 to 0.15625
- w_value: float32 [1536, 1536], P(('blk', 'head')), may hold values from -0.15625 to 0.15625
- w_gate_out: float32 [1536, 1536], P(('blk', 'head')), may hold values from -0.15625 to 0.15625
- w_forget: float32 [1536, 24], P(('blk', 'head')), may hold values from -0.15625 to 0.15625
- forget_bias: float32 [24], replicated, may hold values from 3 to 10
- w_output: float32 [1536, 1536], P(('blk', 'head')), may hold values from -1.75 to 1.75
- norm2_gain: float32 [1536], P(('blk', 'head')), may hold values from 0.5 to 1.5
- w_gate: float32 [1536, 4096], P(('blk', 'head')), may hold values from -0.15625 to 0.15625
- w_up: float32 [1536, 4096], P(('blk', 'head')), may hold values from -0.15625 to 0.15625
- w_down: float32 [1536, 4096], P(('blk', 'head')), may hold values from -0.09375 to 0.09375
- cotangent: bfloat16 [16384, 1536], P(('blk', 'head')), may hold values from -6 to 6
Outputs:
- tokens_out: bfloat16 [16384, 1536], P(('blk', 'head'))
- tokens_grad: float32 [16384, 1536], P(('blk', 'head'))
- norm1_gain_grad: float32 [1536], P(('blk', 'head'))
- w_query_grad: float32 [1536, 1536], P(('blk', 'head'))
- w_key_grad: float32 [1536, 1536], P(('blk', 'head'))
- w_value_grad: float32 [1536, 1536], P(('blk', 'head'))
- w_gate_out_grad: float32 [1536, 1536], P(('blk', 'head'))
- w_forget_grad: float32 [1536, 24], P(('blk', 'head'))
- forget_bias_grad: float32 [24], replicated
- w_output_grad: float32 [1536, 1536], P(('blk', 'head'))
- norm2_gain_grad: float32 [1536], P(('blk', 'head'))
- w_gate_grad: float32 [1536, 4096], P(('blk', 'head'))
- w_up_grad: float32 [1536, 4096], P(('blk', 'head'))
- w_down_grad: float32 [1536, 4096], P(('blk', 'head'))
Inputs may be any that keep to these rules, and one draw needn't show every extreme that they name: `segment`: segment numbers never fall along the tokens and every number occurs; a document has 1 to 2000 tokens and one has exactly 2000.
All inputs are finite; a program needn't handle non-finite values.
Results may differ from a plain program's by a relative error of at most 0.014.
The roundings to bfloat16 on the way count: a program that leaves them out, or rounds other values in their place, can miss the bound.
Values may be sent and summed in bfloat16 or wider, within the bound.
A program may use at most 384 MiB of HBM per device.

v0:
```python
import jax
import jax.numpy as jnp
from jax import lax
from jax.sharding import PartitionSpec as P

epsilon = 1e-06


def passed_along(array, axis, by):
    peers = lax.axis_size(axis)
    pairs = [(i, i + by) for i in range(peers) if 0 <= i + by < peers]
    return lax.ppermute(array, axis, pairs)


def normalize(hidden):
    factor = lax.rsqrt(jnp.mean(hidden * hidden, axis=1, keepdims=True) + epsilon)
    return (hidden * factor, factor)


def norm_back(grad_hat, normed, factor):
    return factor * (grad_hat - normed * jnp.mean(grad_hat * normed, axis=1, keepdims=True))


def times_rows(operand, weight):
    return lax.dot_general(
        operand, weight, (((1,), (1,)), ((), ())), preferred_element_type=jnp.float32
    )


def over_tokens(operand, other_side):
    return lax.dot_general(
        operand, other_side, (((0,), (0,)), ((), ())), preferred_element_type=jnp.float32
    )


def masked_scores(
    query_block, key_window, sums_query, sums_key, marks_query, marks_key, block_rows
):
    scaling = query_block.shape[2] ** (-0.5)
    logits = (
        jnp.einsum("qhd,khd->hqk", query_block, key_window, preferred_element_type=jnp.float32)
        * scaling
    )
    decays = sums_query.T[:, :, None] - sums_key.T[:, None, :]
    shape_pair = (query_block.shape[0], key_window.shape[0])
    query_place = lax.broadcasted_iota(jnp.int32, shape_pair, 0)
    key_place = lax.broadcasted_iota(jnp.int32, shape_pair, 1)
    allowed = (marks_query[:, None] == marks_key[None, :]) & (key_place <= query_place + block_rows)
    return jnp.where(allowed[None], logits + decays, -jnp.inf)


def body(
    tokens,
    segment,
    norm1_gain,
    w_query,
    w_key,
    w_value,
    w_gate_out,
    w_forget,
    forget_bias,
    w_output,
    norm2_gain,
    w_gate,
    w_up,
    w_down,
    cotangent,
):
    token_rows, model_width = tokens.shape
    group_count = lax.axis_size("head")
    head_count = forget_bias.shape[0]
    local_heads = head_count // group_count
    head_width = model_width // head_count
    local_width = local_heads * head_width
    block_rows = token_rows * group_count
    query_rows = min(512, block_rows)
    block_count = block_rows // query_rows
    key_rows = block_rows + query_rows
    first_gain_low = norm1_gain.astype(jnp.bfloat16)
    query_weight_low = w_query.astype(jnp.bfloat16)
    key_weight_low = w_key.astype(jnp.bfloat16)
    value_weight_low = w_value.astype(jnp.bfloat16)
    output_gate_low = w_gate_out.astype(jnp.bfloat16)
    forget_weight_low = w_forget.astype(jnp.bfloat16)
    second_gain_low = norm2_gain.astype(jnp.bfloat16)
    output_weight_low = w_output.astype(jnp.bfloat16)
    gate_weight_low = w_gate.astype(jnp.bfloat16)
    up_weight_low = w_up.astype(jnp.bfloat16)
    down_weight_low = w_down.astype(jnp.bfloat16)
    inputs = tokens.astype(jnp.float32)
    normed1, factor1 = normalize(inputs)
    pieces = (
        lax.all_gather(first_gain_low, ("blk", "head"), axis=0, tiled=True),
        lax.all_gather(query_weight_low, ("blk", "head"), axis=0, tiled=True),
        lax.all_gather(key_weight_low, ("blk", "head"), axis=0, tiled=True),
        lax.all_gather(value_weight_low, ("blk", "head"), axis=0, tiled=True),
        lax.all_gather(output_gate_low, ("blk", "head"), axis=0, tiled=True),
        lax.all_gather(forget_weight_low, ("blk", "head"), axis=0, tiled=True),
    )
    scaled = (normed1 * pieces[0].astype(jnp.float32)).astype(jnp.bfloat16)
    query_raw, key_raw, value_raw, gate_raw, forget_raw = tuple(
        (jnp.dot(scaled, member, preferred_element_type=jnp.float32) for member in pieces[1:])
    )
    forget_full = forget_raw + forget_bias[None, :]
    query_low = query_raw.astype(jnp.bfloat16).reshape(token_rows, group_count, local_width)
    key_low = key_raw.astype(jnp.bfloat16).reshape(token_rows, group_count, local_width)
    value_low = value_raw.astype(jnp.bfloat16).reshape(token_rows, group_count, local_width)
    forget_low = forget_full.astype(jnp.bfloat16).reshape(token_rows, group_count, local_heads)
    query_heads, key_heads, value_heads, forget_heads = (
        lax.all_to_all(query_low, "head", split_axis=1, concat_axis=0, tiled=True),
        lax.all_to_all(key_low, "head", split_axis=1, concat_axis=0, tiled=True),
        lax.all_to_all(value_low, "head", split_axis=1, concat_axis=0, tiled=True),
        lax.all_to_all(forget_low, "head", split_axis=1, concat_axis=0, tiled=True),
    )
    query_heads = query_heads.reshape(block_rows, local_heads, head_width)
    key_heads = key_heads.reshape(block_rows, local_heads, head_width)
    value_heads = value_heads.reshape(block_rows, local_heads, head_width)
    forget_heads = forget_heads.reshape(block_rows, local_heads)
    segment_plus = segment + 1
    earlier_key, earlier_value, earlier_forget, earlier_segment = passed_along(
        (key_heads, value_heads, forget_heads, segment_plus), "blk", 1
    )
    key_joined = jnp.concatenate([earlier_key, key_heads], axis=0)
    value_joined = jnp.concatenate([earlier_value, value_heads], axis=0)
    forget_joined = jnp.concatenate([earlier_forget, forget_heads], axis=0).astype(jnp.float32)
    segment_joined = jnp.concatenate([earlier_segment, segment_plus], axis=0)
    decay_sums = jnp.cumsum(jax.nn.log_sigmoid(forget_joined), axis=0)

    def windows(offset):
        query_block = lax.dynamic_slice_in_dim(query_heads, offset, query_rows, 0)
        key_window = lax.dynamic_slice_in_dim(key_joined, offset, key_rows, 0)
        value_window = lax.dynamic_slice_in_dim(value_joined, offset, key_rows, 0)
        scores = masked_scores(
            query_block,
            key_window,
            lax.dynamic_slice_in_dim(decay_sums, offset + block_rows, query_rows, 0),
            lax.dynamic_slice_in_dim(decay_sums, offset, key_rows, 0),
            lax.dynamic_slice_in_dim(segment_joined, offset + block_rows, query_rows, 0),
            lax.dynamic_slice_in_dim(segment_joined, offset, key_rows, 0),
            block_rows,
        )
        return (query_block, key_window, value_window, scores)

    def attend(number):
        query_block, key_window, value_window, scores = windows(number * query_rows)
        largest = jnp.max(scores, axis=2, keepdims=True)
        weights = jnp.exp(scores - largest)
        normalizer = jnp.sum(weights, axis=2, keepdims=True)
        probabilities = (weights / normalizer).astype(jnp.bfloat16)
        mixed = jnp.einsum(
            "hqk,khd->qhd", probabilities, value_window, preferred_element_type=jnp.float32
        )
        return (mixed.astype(jnp.bfloat16), (largest + jnp.log(normalizer))[:, :, 0].T)

    attended_heads, log_norm = lax.map(attend, jnp.arange(block_count, dtype=jnp.int32))
    log_norm = log_norm.reshape(block_rows, local_heads)
    attended = lax.all_to_all(
        attended_heads.reshape(block_rows, 1, local_width),
        "head",
        split_axis=0,
        concat_axis=1,
        tiled=True,
    ).reshape(token_rows, model_width)
    opened = jax.nn.sigmoid(gate_raw)
    attended_wide = attended.astype(jnp.float32)
    gated = (opened * attended_wide).astype(jnp.bfloat16)
    second_gain, output_weight, gate_weight, up_weight, down_weight = (
        lax.all_gather(second_gain_low, ("blk", "head"), axis=0, tiled=True),
        lax.all_gather(output_weight_low, ("blk", "head"), axis=0, tiled=True),
        lax.all_gather(gate_weight_low, ("blk", "head"), axis=0, tiled=True),
        lax.all_gather(up_weight_low, ("blk", "head"), axis=0, tiled=True),
        lax.all_gather(down_weight_low, ("blk", "head"), axis=0, tiled=True),
    )
    middle = inputs + times_rows(gated, output_weight)
    normed2, factor2 = normalize(middle)
    input2 = (normed2 * second_gain.astype(jnp.float32)).astype(jnp.bfloat16)
    gate_act = jnp.dot(input2, gate_weight, preferred_element_type=jnp.float32)
    up_act = jnp.dot(input2, up_weight, preferred_element_type=jnp.float32)
    opening = jax.nn.sigmoid(gate_act)
    hidden = (gate_act * opening * up_act).astype(jnp.bfloat16)
    result = (middle + times_rows(hidden, down_weight)).astype(jnp.bfloat16)
    second_gain, output_weight, gate_weight, up_weight, down_weight = (
        lax.all_gather(second_gain_low, ("blk", "head"), axis=0, tiled=True),
        lax.all_gather(output_weight_low, ("blk", "head"), axis=0, tiled=True),
        lax.all_gather(gate_weight_low, ("blk", "head"), axis=0, tiled=True),
        lax.all_gather(up_weight_low, ("blk", "head"), axis=0, tiled=True),
        lax.all_gather(down_weight_low, ("blk", "head"), axis=0, tiled=True),
    )
    grad_hidden = jnp.dot(cotangent, down_weight, preferred_element_type=jnp.float32)
    grad_gate_act = (grad_hidden * up_act * opening * (1.0 + gate_act * (1.0 - opening))).astype(
        jnp.bfloat16
    )
    grad_up_act = (grad_hidden * gate_act * opening).astype(jnp.bfloat16)
    grad_input2 = times_rows(grad_gate_act, gate_weight) + times_rows(grad_up_act, up_weight)
    grad_second_gain = jnp.sum(normed2 * grad_input2, axis=0)
    grad_middle = cotangent.astype(jnp.float32) + norm_back(
        grad_input2 * second_gain.astype(jnp.float32), normed2, factor2
    )
    grad_branch = grad_middle.astype(jnp.bfloat16)
    second_grads = (
        lax.psum_scatter(
            over_tokens(grad_branch, gated), ("blk", "head"), scatter_dimension=0, tiled=True
        ),
        lax.psum_scatter(
            over_tokens(input2, grad_gate_act), ("blk", "head"), scatter_dimension=0, tiled=True
        ),
        lax.psum_scatter(
            over_tokens(input2, grad_up_act), ("blk", "head"), scatter_dimension=0, tiled=True
        ),
        lax.psum_scatter(
            over_tokens(cotangent, hidden), ("blk", "head"), scatter_dimension=0, tiled=True
        ),
    )
    output_total, gate_total, up_total, down_total = second_grads
    grad_gated = jnp.dot(grad_branch, output_weight, preferred_element_type=jnp.float32)
    grad_attended = (grad_gated * opened).astype(jnp.bfloat16)
    grad_gate_pre = (grad_gated * attended_wide * opened * (1.0 - opened)).astype(jnp.bfloat16)
    grad_heads = lax.all_to_all(
        grad_attended.reshape(token_rows, group_count, local_width),
        "head",
        split_axis=1,
        concat_axis=0,
        tiled=True,
    ).reshape(block_rows, local_heads, head_width)
    scaling = head_width ** (-0.5)

    def attend_back(number, carry):
        query_grad, key_grad, value_grad, decay_grad = carry
        offset = number * query_rows
        query_block, key_window, value_window, scores = windows(offset)
        norm_block = lax.dynamic_slice_in_dim(log_norm, offset, query_rows, 0)
        probabilities = jnp.exp(scores - norm_block.T[:, :, None])
        grad_block = lax.dynamic_slice_in_dim(grad_heads, offset, query_rows, 0)
        grad_prob = jnp.einsum(
            "qhd,khd->hqk", grad_block, value_window, preferred_element_type=jnp.float32
        )
        inner = jnp.sum(probabilities * grad_prob, axis=2, keepdims=True)
        grad_score = probabilities * (grad_prob - inner)
        grad_low = grad_score.astype(jnp.bfloat16)
        query_part = (
            jnp.einsum("hqk,khd->qhd", grad_low, key_window, preferred_element_type=jnp.float32)
            * scaling
        )
        key_part = (
            jnp.einsum("hqk,qhd->khd", grad_low, query_block, preferred_element_type=jnp.float32)
            * scaling
        )
        value_part = jnp.einsum(
            "hqk,qhd->khd",
            probabilities.astype(jnp.bfloat16),
            grad_block,
            preferred_element_type=jnp.float32,
        )
        query_grad = lax.dynamic_update_slice_in_dim(query_grad, query_part, offset, 0)
        key_grad = lax.dynamic_update_slice_in_dim(
            key_grad, lax.dynamic_slice_in_dim(key_grad, offset, key_rows, 0) + key_part, offset, 0
        )
        value_grad = lax.dynamic_update_slice_in_dim(
            value_grad,
            lax.dynamic_slice_in_dim(value_grad, offset, key_rows, 0) + value_part,
            offset,
            0,
        )
        decay_grad = lax.dynamic_update_slice_in_dim(
            decay_grad,
            lax.dynamic_slice_in_dim(decay_grad, offset, key_rows, 0)
            - jnp.sum(grad_score, axis=1).T,
            offset,
            0,
        )
        decay_grad = lax.dynamic_update_slice_in_dim(
            decay_grad,
            lax.dynamic_slice_in_dim(decay_grad, offset + block_rows, query_rows, 0)
            + jnp.sum(grad_score, axis=2).T,
            offset + block_rows,
            0,
        )
        return (query_grad, key_grad, value_grad, decay_grad)

    initial_back = (
        jnp.zeros((block_rows, local_heads, head_width), jnp.float32),
        jnp.zeros((2 * block_rows, local_heads, head_width), jnp.float32),
        jnp.zeros((2 * block_rows, local_heads, head_width), jnp.float32),
        jnp.zeros((2 * block_rows, local_heads), jnp.float32),
    )
    query_grad, key_grad, value_grad, decay_grad = lax.fori_loop(
        0, block_count, attend_back, initial_back
    )
    logf_grad = lax.cumsum(decay_grad, axis=0, reverse=True)
    later_key, later_value, later_logf = (
        passed_along(key_grad[:block_rows].astype(jnp.bfloat16), "blk", -1).astype(jnp.float32),
        passed_along(value_grad[:block_rows].astype(jnp.bfloat16), "blk", -1).astype(jnp.float32),
        passed_along(logf_grad[:block_rows].astype(jnp.bfloat16), "blk", -1).astype(jnp.float32),
    )
    key_total = (key_grad[block_rows:] + later_key).astype(jnp.bfloat16)
    value_total = (value_grad[block_rows:] + later_value).astype(jnp.bfloat16)
    forget_total = (
        (logf_grad[block_rows:] + later_logf) * jax.nn.sigmoid(-forget_heads.astype(jnp.float32))
    ).astype(jnp.bfloat16)
    query_total = query_grad.astype(jnp.bfloat16)
    query_back, key_back, value_back, forget_back = (
        lax.all_to_all(
            query_total.reshape(block_rows, 1, local_width),
            "head",
            split_axis=0,
            concat_axis=1,
            tiled=True,
        ),
        lax.all_to_all(
            key_total.reshape(block_rows, 1, local_width),
            "head",
            split_axis=0,
            concat_axis=1,
            tiled=True,
        ),
        lax.all_to_all(
            value_total.reshape(block_rows, 1, local_width),
            "head",
            split_axis=0,
            concat_axis=1,
            tiled=True,
        ),
        lax.all_to_all(
            forget_total.reshape(block_rows, 1, local_heads),
            "head",
            split_axis=0,
            concat_axis=1,
            tiled=True,
        ),
    )
    query_back = query_back.reshape(token_rows, model_width)
    key_back = key_back.reshape(token_rows, model_width)
    value_back = value_back.reshape(token_rows, model_width)
    forget_back = forget_back.reshape(token_rows, head_count)
    first_gain, query_weight, key_weight, value_weight, output_gate_weight, forget_weight = (
        lax.all_gather(first_gain_low, ("blk", "head"), axis=0, tiled=True),
        lax.all_gather(query_weight_low, ("blk", "head"), axis=0, tiled=True),
        lax.all_gather(key_weight_low, ("blk", "head"), axis=0, tiled=True),
        lax.all_gather(value_weight_low, ("blk", "head"), axis=0, tiled=True),
        lax.all_gather(output_gate_low, ("blk", "head"), axis=0, tiled=True),
        lax.all_gather(forget_weight_low, ("blk", "head"), axis=0, tiled=True),
    )
    input1 = (normed1 * first_gain.astype(jnp.float32)).astype(jnp.bfloat16)
    grad_input1 = (
        times_rows(query_back, query_weight)
        + times_rows(key_back, key_weight)
        + times_rows(value_back, value_weight)
    )
    grad_input1 = (
        grad_input1
        + times_rows(grad_gate_pre, output_gate_weight)
        + times_rows(forget_back, forget_weight)
    )
    grad_first_gain = jnp.sum(normed1 * grad_input1, axis=0)
    tokens_grad = grad_middle + norm_back(
        grad_input1 * first_gain.astype(jnp.float32), normed1, factor1
    )
    bias_local = jnp.sum(forget_back.astype(jnp.float32), axis=0)
    first_grads = (
        lax.psum_scatter(
            over_tokens(input1, query_back), ("blk", "head"), scatter_dimension=0, tiled=True
        ),
        lax.psum_scatter(
            over_tokens(input1, key_back), ("blk", "head"), scatter_dimension=0, tiled=True
        ),
        lax.psum_scatter(
            over_tokens(input1, value_back), ("blk", "head"), scatter_dimension=0, tiled=True
        ),
        lax.psum_scatter(
            over_tokens(input1, grad_gate_pre), ("blk", "head"), scatter_dimension=0, tiled=True
        ),
        lax.psum_scatter(
            over_tokens(input1, forget_back), ("blk", "head"), scatter_dimension=0, tiled=True
        ),
    )
    query_sum, key_sum, value_sum, gate_out_sum, forget_sum = first_grads
    gain1_whole, gain2_whole, bias_total = lax.psum(
        (grad_first_gain, grad_second_gain, bias_local), ("blk", "head")
    )
    share_rows = model_width // lax.axis_size(("blk", "head"))
    share_start = lax.axis_index(("blk", "head")) * share_rows
    gain1_total = lax.dynamic_slice_in_dim(gain1_whole, share_start, share_rows, 0)
    gain2_total = lax.dynamic_slice_in_dim(gain2_whole, share_start, share_rows, 0)
    return (
        result,
        tokens_grad,
        gain1_total,
        query_sum,
        key_sum,
        value_sum,
        gate_out_sum,
        forget_sum,
        bias_total,
        output_total,
        gain2_total,
        gate_total,
        up_total,
        down_total,
    )


def solution(mesh):
    placed = (
        P(("blk", "head"), None),
        P("blk"),
        P(("blk", "head")),
        P(("blk", "head"), None),
        P(("blk", "head"), None),
        P(("blk", "head"), None),
        P(("blk", "head"), None),
        P(("blk", "head"), None),
        P(),
        P(("blk", "head"), None),
        P(("blk", "head")),
        P(("blk", "head"), None),
        P(("blk", "head"), None),
        P(("blk", "head"), None),
        P(("blk", "head"), None),
    )
    return jax.shard_map(
        body,
        mesh=mesh,
        in_specs=placed,
        out_specs=(
            P(("blk", "head"), None),
            P(("blk", "head"), None),
            P(("blk", "head")),
            P(("blk", "head"), None),
            P(("blk", "head"), None),
            P(("blk", "head"), None),
            P(("blk", "head"), None),
            P(("blk", "head"), None),
            P(),
            P(("blk", "head"), None),
            P(("blk", "head")),
            P(("blk", "head"), None),
            P(("blk", "head"), None),
            P(("blk", "head"), None),
        ),
        check_vma=False,
    )
```

profile of v0, /device:TPU:0, one launch (start us, length us, event | category | flops | bytes accessed | tf_op | source)
XLA Modules:
  0.0 2825.7 jit_solution(7312303872974199361)
XLA Ops:
  18.3 42.1 %all-reduce.3 = (bf16[1536]{0:T(1024)(128)(2,1)S(1)}, bf16[1536]{0:T(1024)(128)(2,1)}) all-reduce(bf16[1536]{0:T(1024)(128)(2,1)S(1)} %dynamic-update-slice, bf16[1536]{0:T(1024)(128)(2,1)S(1)} %dynamic-update-slice.1), channel_id=1, replica_groups=mesh['blk'=8,'head'=4] {'blk','head'}, use_global_device_ids=true, to_apply=%add | all-reduce | flops 3072 | bytes 12288
  60.4 42.0 %all-gather = bf16[32,48,24]{1,2,0:T(8,128)(2,1)S(1)} all-gather(bf16[1,48,24]{1,2,0:T(8,128)(2,1)S(1)} %convert_bitcast_fusion.1), channel_id=1, replica_groups=mesh['blk'=8,'head'=4] {'blk','head'}, dimensions={0}, use_global_device_ids=true | all-gather | bytes 76032 | tf_op jit(solution)/shard_map/all_gather | solution.py:98
  117.6 31.7 %all-gather.16.cloned.1.call-done = bf16[1536,1536]{1,0:T(8,128)(2,1)} async-done(((bf16[48,1536]{1,0:T(8,128)(2,1)}), bf16[1536,1536]{1,0:T(8,128)(2,1)}) %all-gather.16.cloned.1.call-update) | async-done | bytes 4718608 | tf_op jit(solution)/shard_map/all_gather | solution.py:95
  172.2 56.6 %all-gather.14.cloned.1.call-done = bf16[1536,1536]{1,0:T(8,128)(2,1)} async-done(((bf16[48,1536]{1,0:T(8,128)(2,1)}), bf16[1536,1536]{1,0:T(8,128)(2,1)}) %all-gather.14.cloned.1.call-update) | async-done | bytes 4718608 | tf_op jit(solution)/shard_map/all_gather | solution.py:94
  260.5 38.0 %collective-permute-done.1 = s32[2048]{0:T(1024)S(1)} collective-permute-done((s32[2048]{0:T(1024)S(1)}, s32[2048]{0:T(1024)S(1)}, u32[]{:S(2)}, u32[]{:S(2)}) %collective-permute-start.1) | collective-permute-done | bytes 8224 | tf_op jit(solution)/shard_map/ppermute | solution.py:12
  315.7 208.8 %while.35 = (s32[]{:T(128)}, bf16[4,512,6,64]{1,3,2,0:T(8,128)(2,1)}, f32[4,512,6]{1,2,0:T(8,128)}, s32[4]{0:T(128)S(1)}, bf16[4096,6,64]{0,2,1:T(8,128)(2,1)}, ...) while((s32[]{:T(128)}, ...), condition=%wide.region_6.7_spmd, body=%wide.region_3.6_spmd.sunk | while | flops 2158949888 | bytes 117485888 | solution.py:155
  543.8 28.3 %all-to-all-done.4 = bf16[4,2,98304]{2,1,0:T(2,128)(2,1)} async-done(((bf16[4,2,98304]{2,1,0:T(2,128)(2,1)}), bf16[4,2,98304]{2,1,0:T(2,128)(2,1)}, u32[]{:S(2)}, u32[]{:S(2)}) %all-to-all-start.4) | async-done | bytes 1572896 | tf_op jit(solution)/shard_map/all_to_all | solution.py:157
  618.5 58.5 %all-gather.24.cloned.1.call-done = bf16[1536,4096]{1,0:T(8,128)(2,1)} async-done(((bf16[48,4096]{1,0:T(8,128)(2,1)}), bf16[1536,4096]{1,0:T(8,128)(2,1)}) %all-gather.24.cloned.1.call-update) | async-done | bytes 12582928 | tf_op jit(solution)/shard_map/all_gather | solution.py:172
  677.0 19.3 multiply_convert_fusion
  731.8 20.0 all-to-all-done.5
  763.9 430.7 %while.36 = (s32[]{:T(128)}, bf16[2048,6,64]{0,2,1:T(8,128)(2,1)}, f32[4096,6,64]{0,2,1:T(8,128)}, f32[4096,6,64]{0,2,1:T(8,128)}, f32[4096,6]{0,1:T(8,128)S(1)}...) while((s32[]{:T(128)}, bf16[2048,6,64]{0,2,1:T(8,128)(2,1)}, ...), condition=%wide.region_13.14_spmd, body=%wide.region_9.13_spmd.sunk | while | flops 5142476288 | bytes 263229760 | solution.py:286
  780.4 26.2 multiply_reduce_fusion.5
  806.6 26.1 fusion.206
  887.9 26.2 multiply_reduce_fusion.5
  914.2 26.1 fusion.206
  995.5 26.2 multiply_reduce_fusion.5
  1021.7 26.1 fusion.206
  1103.0 26.2 multiply_reduce_fusion.5
  1129.1 26.1 fusion.206
  1240.0 22.5 all_to_all.145
  1279.8 37.2 %collective-permute-done.4 = bf16[2048,6,64]{0,2,1:T(8,128)(2,1)S(1)} collective-permute-done((bf16[2048,6,64]{0,2,1:T(8,128)(2,1)S(1)}, bf16[2048,6,64]{0,2,1:T(8,128)(2,1)S(1)}, u32[]{:S(2)}, u32[]{:S(2)}) %collective-permute-start.4) | collective-permute-done | bytes 1572896 | tf_op jit(solution)/shard_map/ppermute | solution.py:12
  1325.7 23.7 all_to_all.146
  1366.5 55.1 %collective-permute-done.5 = bf16[2048,6,64]{0,2,1:T(8,128)(2,1)S(1)} collective-permute-done((bf16[2048,6,64]{0,2,1:T(8,128)(2,1)S(1)}, bf16[2048,6,64]{0,2,1:T(8,128)(2,1)S(1)}, u32[]{:S(2)}, u32[]{:S(2)}) %collective-permute-start.5) | collective-permute-done | bytes 1572896 | tf_op jit(solution)/shard_map/ppermute | solution.py:12
  1430.4 28.9 %all_to_all.147 = bf16[4,2,98304]{2,1,0:T(2,128)(2,1)S(1)} all-to-all(bf16[4,2,98304]{2,1,0:T(2,128)(2,1)} %reshape.293), channel_id=1, replica_groups=mesh['blk'=8,'head'=4] {'head'}, dimensions={0} | all-to-all | bytes 3145728 | tf_op jit(solution)/shard_map/all_to_all | solution.py:316
  1518.6 25.4 copy.152
  1577.9 53.1 %all-reduce.2 = (f32[1536]{0:T(1024)S(1)}, f32[24]{0:T(128)}, f32[1536]{0:T(1024)S(1)}) all-reduce(f32[1536]{0:T(1024)S(1)} %get-tuple-element.546, f32[24]{0:T(128)S(1)} %reduce_sum.131, f32[1536]{0:T(1024)S(1)} %copy-done.48), channel_id=1, replica_groups=mesh['blk'=8,'head'=4] {'blk','head'}, use_global_device_ids=true, to_apply=%region_18.19 | all-reduce | flops 3096 | bytes 24768 | tf_op jit(solution)/shard_map/psum | solution.py:377
  1637.5 141.0 %reduce-scatter.14.cloned.1.call-done = f32[48,1536]{1,0:T(8,128)} async-done(((f32[1536,1536]{1,0:T(8,128)}), f32[48,1536]{1,0:T(8,128)}) %reduce-scatter.14.cloned.1.call-update) | async-done | bytes 294928 | tf_op jit(solution)/shard_map/reduce_scatter | solution.py:360
  1778.5 142.1 %reduce-scatter.16.cloned.1.call-done = f32[48,1536]{1,0:T(8,128)} async-done(((f32[1536,1536]{1,0:T(8,128)}), f32[48,1536]{1,0:T(8,128)}) %reduce-scatter.16.cloned.1.call-update) | async-done | bytes 294928 | tf_op jit(solution)/shard_map/reduce_scatter | solution.py:363
  1920.6 141.0 %reduce-scatter.18.cloned.1.call-done = f32[48,1536]{1,0:T(8,128)} async-done(((f32[1536,1536]{1,0:T(8,128)}), f32[48,1536]{1,0:T(8,128)}) %reduce-scatter.18.cloned.1.call-update) | async-done | bytes 294928 | tf_op jit(solution)/shard_map/reduce_scatter | solution.py:366
  2061.6 252.4 %reduce-scatter.24.cloned.1.call-done = f32[48,4096]{1,0:T(8,128)} async-done(((f32[1536,4096]{1,0:T(8,128)}), f32[48,4096]{1,0:T(8,128)}) %reduce-scatter.24.cloned.1.call-update) | async-done | bytes 786448 | tf_op jit(solution)/shard_map/reduce_scatter | solution.py:204
  2314.0 251.9 %reduce-scatter.26.cloned.1.call-done = f32[48,4096]{1,0:T(8,128)} async-done(((f32[1536,4096]{1,0:T(8,128)}), f32[48,4096]{1,0:T(8,128)}) %reduce-scatter.26.cloned.1.call-update) | async-done | bytes 786448 | tf_op jit(solution)/shard_map/reduce_scatter | solution.py:207
  2565.9 253.0 %reduce-scatter.30.cloned.1.call-done = f32[48,4096]{1,0:T(8,128)} async-done(((f32[1536,4096]{1,0:T(8,128)}), f32[48,4096]{1,0:T(8,128)}) %reduce-scatter.30.cloned.1.call-update) | async-done | bytes 786448
  (429 shorter events, 832.9 us)
Async XLA Ops:
  7.2 100.5 %all-gather.12.cloned.1.call-start = ((), (), s32[]{:S(2)}) async-start(), calls=%async_computation.20 | async-start | bytes 4866048 | tf_op jit(solution)/shard_map/all_gather | solution.py:96
  9.1 140.3 %all-gather.16.cloned.1.call-start = ((), (), s32[]{:S(2)}) async-start(), calls=%async_computation.22 | async-start | bytes 4866048 | tf_op jit(solution)/shard_map/all_gather | solution.py:95
  10.9 218.0 %all-gather.14.cloned.1.call-start = ((), (), s32[]{:S(2)}) async-start(), calls=%async_computation.21 | async-start | bytes 4866048 | tf_op jit(solution)/shard_map/all_gather | solution.py:94
  12.6 567.0 %all-gather.10.cloned.1.call-start = ((), (), s32[]{:S(2)}) async-start(), calls=%async_computation.19 | async-start | bytes 4866048 | tf_op jit(solution)/shard_map/all_gather | solution.py:97
  14.3 572.5 %all-gather.18.cloned.1.call-start = ((), (), s32[]{:S(2)}) async-start(), calls=%async_computation.23 | async-start | bytes 4866048 | tf_op jit(solution)/shard_map/all_gather | solution.py:169
  16.0 578.1 %all-gather.20.cloned.1.call-start = ((), (), s32[]{:S(2)}) async-start(), calls=%async_computation.24 | async-start | bytes 12976128 | tf_op jit(solution)/shard_map/all_gather | solution.py:170
  16.9 589.5 %all-gather.22.cloned.1.call-start = ((), (), s32[]{:S(2)}) async-start(), calls=%async_computation.25 | async-start | bytes 12976128 | tf_op jit(solution)/shard_map/all_gather | solution.py:171
  104.4 9.6 all-to-all-start.3
  114.0 184.8 %copy-start.36 = (bf16[512,4,6]{0,2,1:T(8,128)(2,1)}, bf16[512,4,6]{0,2,1:T(8,128)(2,1)S(1)}, u32[]{:S(2)}) copy-start(bf16[512,4,6]{0,2,1:T(8,128)(2,1)S(1)} %all-to-all-done.3) | copy-start | bytes 73732
  114.0 41.6 %all-to-all-start = ((bf16[512,4,384]{2,0,1:T(8,128)(2,1)}), bf16[512,4,384]{2,0,1:T(8,128)(2,1)S(1)}, u32[]{:S(2)}, u32[]{:S(2)}) async-start(bf16[512,4,384]{2,0,1:T(8,128)(2,1)} %bitcast.236), calls=%async_computation | async-start | bytes 3145728 | tf_op jit(solution)/shard_map/all_to_all | solution.py:112
  156.8 78.4 %all-to-all-start.2 = ((bf16[512,4,384]{2,0,1:T(8,128)(2,1)}), bf16[512,4,384]{2,0,1:T(8,128)(2,1)S(1)}, u32[]{:S(2)}, u32[]{:S(2)}) async-start(bf16[512,4,384]{2,0,1:T(8,128)(2,1)} %bitcast.234), calls=%async_computation.2 | async-start | bytes 3145728 | tf_op jit(solution)/shard_map/all_to_all | solution.py:111
  168.0 138.6 %collective-permute-start = (bf16[2048,6,64]{0,2,1:T(8,128)(2,1)}, bf16[2048,6,64]{0,2,1:T(8,128)(2,1)}, u32[]{:S(2)}, u32[]{:S(2)}) collective-permute-start(bf16[2048,6,64]{0,2,1:T(8,128)(2,1)} %reshape.250), channel_id=1, source_target_pairs={{0,4},{4,8},{8,12},{12,16},{16,20},{20,24},{24,28},{1,5},{5,9},{9,... | collective-permute-start | bytes 4718600 | tf_op jit(solution)/shard_map/ppermute | solution.py:12
  236.3 64.9 %all-to-all-start.1 = ((bf16[512,4,384]{2,0,1:T(8,128)(2,1)}), bf16[512,4,384]{2,0,1:T(8,128)(2,1)S(1)}, u32[]{:S(2)}, u32[]{:S(2)}) async-start(bf16[512,4,384]{2,0,1:T(8,128)(2,1)} %bitcast.193), calls=%async_computation.1 | async-start | bytes 3145728 | tf_op jit(solution)/shard_map/all_to_all | solution.py:110
  239.8 437.1 %all-gather.24.cloned.1.call-start = ((), (), s32[]{:S(2)}) async-start(), calls=%async_computation.26 | async-start | bytes 12976128 | tf_op jit(solution)/shard_map/all_gather | solution.py:172
  247.7 62.1 %collective-permute-start.2 = (bf16[2048,6,64]{0,2,1:T(8,128)(2,1)}, bf16[2048,6,64]{0,2,1:T(8,128)(2,1)}, u32[]{:S(2)}, u32[]{:S(2)}) collective-permute-start(bf16[2048,6,64]{0,2,1:T(8,128)(2,1)} %reshape.254), channel_id=1, source_target_pairs={{0,4},{4,8},{8,12},{12,16},{16,20},{20,24},{24,28},{1,5},{5,9},{9,... | collective-permute-start | bytes 4718600 | tf_op jit(solution)/shard_map/ppermute | solution.py:12
  252.0 46.4 %collective-permute-start.1 = (s32[2048]{0:T(1024)S(1)}, s32[2048]{0:T(1024)S(1)}, u32[]{:S(2)}, u32[]{:S(2)}) collective-permute-start(s32[2048]{0:T(1024)S(1)} %broadcast_add_fusion), channel_id=1, source_target_pairs={{0,4},{4,8},{8,12},{12,16},{16,20},{20,24},{24,28},{1,5},{5,9},{9,... | collective-permute-start | bytes 24584 | tf_op jit(solution)/shard_map/ppermute | solution.py:12
  255.3 43.4 %collective-permute-start.3 = (bf16[2048,6]{0,1:T(8,128)(2,1)S(1)}, bf16[2048,6]{0,1:T(8,128)(2,1)S(1)}, u32[]{:S(2)}, u32[]{:S(2)}) collective-permute-start(bf16[2048,6]{0,1:T(8,128)(2,1)S(1)} %bitcast.262), channel_id=1, source_target_pairs={{0,4},{4,8},{8,12},{12,16},{16,20},{20,24},{24,28},{1,5},{5,9},{9,... | collective-permute-start | bytes 73736 | tf_op jit(solution)/shard_map/ppermute | solution.py:12
  539.5 32.7 %all-to-all-start.4 = ((bf16[4,2,98304]{2,1,0:T(2,128)(2,1)}), bf16[4,2,98304]{2,1,0:T(2,128)(2,1)}, u32[]{:S(2)}, u32[]{:S(2)}) async-start(bf16[4,2,98304]{2,1,0:T(2,128)(2,1)} %reshape.287), calls=%async_computation.4 | async-start | bytes 3145728 | tf_op jit(solution)/shard_map/all_to_all | solution.py:157
  728.2 23.6 all-to-all-start.5
  731.7 826.3 %reduce-scatter.28.cloned.1.call-start = ((), (), s32[]{:S(2)}) async-start(), calls=%async_computation.34 | async-start | bytes 811008
  763.9 444.6 %copy-start.37 = (bf16[512,4,6]{0,2,1:T(8,128)(2,1)S(1)}, bf16[512,4,6]{0,2,1:T(8,128)(2,1)}, u32[]{:S(2)}) copy-start(bf16[512,4,6]{0,2,1:T(8,128)(2,1)} %copy-done.36) | copy-start | bytes 73732
  1202.8 5.8 collective-permute-start.6
  1220.2 416.8 %reduce-scatter.20.cloned.1.call-start = ((), (), s32[]{:S(2)}) async-start(), calls=%async_computation.30 | async-start | bytes 9732096 | tf_op jit(solution)/shard_map/reduce_scatter | solution.py:369
  1226.9 410.7 %reduce-scatter.22.cloned.1.call-start = ((), (), s32[]{:S(2)}) async-start(), calls=%async_computation.31 | async-start | bytes 9732096 | tf_op jit(solution)/shard_map/reduce_scatter | solution.py:201
  1235.3 543.2 %reduce-scatter.14.cloned.1.call-start = ((), (), s32[]{:S(2)}) async-start(), calls=%async_computation.27 | async-start | bytes 9732096 | tf_op jit(solution)/shard_map/reduce_scatter | solution.py:360
  1276.1 644.5 %reduce-scatter.16.cloned.1.call-start = ((), (), s32[]{:S(2)}) async-start(), calls=%async_computation.28 | async-start | bytes 9732096 | tf_op jit(solution)/shard_map/reduce_scatter | solution.py:363
  1278.3 38.7 %collective-permute-start.4 = (bf16[2048,6,64]{0,2,1:T(8,128)(2,1)S(1)}, bf16[2048,6,64]{0,2,1:T(8,128)(2,1)S(1)}, u32[]{:S(2)}, u32[]{:S(2)}) collective-permute-start(bf16[2048,6,64]{0,2,1:T(8,128)(2,1)S(1)} %slice.64), channel_id=1, source_target_pairs={{4,0},{8,4},{12,8},{16,12},{20,16},{24,20},{28,24},{5,1},{9,5},{13... | collective-permute-start | bytes 4718600 | tf_op jit(solution)/shard_map/ppermute | solution.py:12
  1363.0 698.6 %reduce-scatter.18.cloned.1.call-start = ((), (), s32[]{:S(2)}) async-start(), calls=%async_computation.29 | async-start | bytes 9732096 | tf_op jit(solution)/shard_map/reduce_scatter | solution.py:366
  1365.2 56.4 %collective-permute-start.5 = (bf16[2048,6,64]{0,2,1:T(8,128)(2,1)S(1)}, bf16[2048,6,64]{0,2,1:T(8,128)(2,1)S(1)}, u32[]{:S(2)}, u32[]{:S(2)}) collective-permute-start(bf16[2048,6,64]{0,2,1:T(8,128)(2,1)S(1)} %slice.63), channel_id=1, source_target_pairs={{4,0},{8,4},{12,8},{16,12},{20,16},{24,20},{28,24},{5,1},{9,5},{13... | collective-permute-start | bytes 4718600 | tf_op jit(solution)/shard_map/ppermute | solution.py:12
  1472.9 841.1 %reduce-scatter.24.cloned.1.call-start = ((), (), s32[]{:S(2)}) async-start(), calls=%async_computation.32 | async-start | bytes 25952256 | tf_op jit(solution)/shard_map/reduce_scatter | solution.py:204
  1488.3 1077.6 %reduce-scatter.26.cloned.1.call-start = ((), (), s32[]{:S(2)}) async-start(), calls=%async_computation.33 | async-start | bytes 25952256 | tf_op jit(solution)/shard_map/reduce_scatter | solution.py:207
  1502.4 1316.6 %reduce-scatter.30.cloned.1.call-start = ((), (), s32[]{:S(2)}) async-start(), calls=%async_computation.35 | async-start | bytes 25952256
  (62 other events, 1075.6 us)
Sparse Core Ops, SparseCore 0:
  11.5 66.8 all-gather.11
  81.9 67.3 all-gather.15
  152.8 75.9 all-gather.13
  232.2 76.2 all-gather.9
  311.8 64.5 all-gather.17
  379.6 94.9 all-gather.19
  478.1 96.9 all-gather.21
  578.5 98.3 all-gather.23
  1220.3 95.1 reduce-scatter.27
  1321.8 172.8 reduce-scatter.19
  1502.2 135.2 reduce-scatter.21
  1643.9 134.6 reduce-scatter.13
  1786.0 134.5 reduce-scatter.15
  1926.9 134.6 reduce-scatter.17
  2069.6 244.3 reduce-scatter.23
  2320.9 245.0 reduce-scatter.25
  2573.9 244.9 reduce-scatter.29
where the time goes:
time: 2840 us; the launch traced here: 2830 us
  waiting for transfers between devices  1510 us (53%)
  matrix products  651 us (23%)
  other arithmetic  227 us (8%)
  blocking collectives  219 us (8%)
  local copies, waits for them, and re-layouts  153 us (5%)
  starting transfers between devices  43.2 us (2%)
    unnamed x19, waiting for transfers between devices  253 us
    reduce_scatter x1, waiting for transfers between devices, body(): lax.psum_scatter(over_tokens(input2, grad_gate_act), ('blk', 'head'), sca...  252 us
    reduce_scatter x1, waiting for transfers between devices, body(): lax.psum_scatter(over_tokens(input2, grad_up_act), ('blk', 'head'), scatt...  252 us
    dot_general x8, matrix products, masked_scores(): jnp.einsum('qhd,khd->hqk', query_block, key_window, preferred_element_typ...  170 us
    reduce_scatter x1, waiting for transfers between devices, body(): lax.psum_scatter(over_tokens(input1, key_back), ('blk', 'head'), scatter_...  142 us
    reduce_scatter x1, waiting for transfers between devices, body(): lax.psum_scatter(over_tokens(input1, value_back), ('blk', 'head'), scatte...  141 us
    reduce_scatter x1, waiting for transfers between devices, body(): lax.psum_scatter(over_tokens(input1, query_back), ('blk', 'head'), scatte...  141 us
    ppermute x7, waiting for transfers between devices, passed_along(): return lax.ppermute(array, axis, pairs)  135 us
  transfers between devices with their start and end apart: 30, of which 17 were waited for; matrix products, arithmetic and copies ran while one was open for 18% of the time, Pallas kernels for 0%

commit v1 on v0

v1 whole, which is shorter than its diff:
```python
import functools

import jax
import jax.numpy as jnp
from jax import lax
from jax.experimental import pallas as pl
from jax.experimental.pallas import tpu as pltpu
from jax.sharding import PartitionSpec as P

epsilon = 1e-06
LANES = 128
Q_TILE = 512
K_TILE = 256
FAR = -1e30
NT = (((1,), (1,)), ((), ()))
NN = (((1,), (0,)), ((), ()))
bf16 = jnp.bfloat16
f32 = jnp.float32


def dot(a, b, dims=NN, **kw):
    return lax.dot_general(a, b, dims, preferred_element_type=f32, **kw)


def passed_along(array, axis, by):
    peers = lax.axis_size(axis)
    pairs = [(i, i + by) for i in range(peers) if 0 <= i + by < peers]
    return lax.ppermute(array, axis, pairs)


def split3(value):
    high = value.astype(bf16)
    rest = value - high.astype(f32)
    mid = rest.astype(bf16)
    low = (rest - mid.astype(f32)).astype(bf16)
    return high, mid, low


def running(value_of, steps, rows, upper):
    place = lax.broadcasted_iota(jnp.int32, (rows, rows), 0)
    other = lax.broadcasted_iota(jnp.int32, (rows, rows), 1)
    tri = jnp.where((other >= place) if upper else (other <= place), 1.0, 0.0).astype(bf16)
    outs = [None] * steps
    carry = jnp.zeros((1, LANES), f32)
    order = range(steps - 1, -1, -1) if upper else range(steps)
    for n in order:
        block = value_of(n)
        total = sum(dot(tri, part) for part in split3(block)) + carry
        outs[n] = total
        carry = total[0:1] if upper else total[rows - 1 : rows]
    return outs, carry


def decay_kernel(local_heads, logf_ref, own_ref, halo_ref):
    rows = 256
    steps = logf_ref.shape[0] // rows
    lane = lax.broadcasted_iota(jnp.int32, (rows, LANES), 1)

    def value_of(n):
        return jnp.where(lane < local_heads, logf_ref[n * rows : (n + 1) * rows, :], 0.0)

    sums, total = running(value_of, steps, rows, False)
    one = jnp.where(lane == 3 * local_heads, 1.0, 0.0)

    def terms(value):
        high, mid, low = split3(value)
        return (
            high.astype(f32)
            + pltpu.roll(mid.astype(f32), local_heads, 1)
            + pltpu.roll(low.astype(f32), 2 * local_heads, 1)
            + one
        ).astype(bf16)

    for n in range(steps):
        own_ref[n * rows : (n + 1) * rows, :] = terms(sums[n])
        halo_ref[n * rows : (n + 1) * rows, :] = terms(sums[n] - total)


def decay_terms(logf, local_heads):
    shape = jax.ShapeDtypeStruct(logf.shape, bf16)
    return pl.pallas_call(
        functools.partial(decay_kernel, local_heads),
        out_shape=(shape, shape),
        name="decay_terms",
    )(logf)


def decay_back_kernel(own_ref, halo_ref, out_ref):
    rows = 256
    steps = own_ref.shape[0] // rows
    own, _ = running(lambda n: own_ref[n * rows : (n + 1) * rows, :], steps, rows, True)
    halo, _ = running(lambda n: halo_ref[n * rows : (n + 1) * rows, :], steps, rows, False)
    for n in range(steps):
        part = slice(n * rows, (n + 1) * rows)
        out_ref[part, :] = own[n] + (halo[n] - halo_ref[part, :])


def decay_back(own, halo):
    return pl.pallas_call(
        decay_back_kernel,
        out_shape=jax.ShapeDtypeStruct(own.shape, f32),
        name="decay_back",
    )(own, halo)


def placing(pair, local_heads, for_query):
    row = lax.broadcasted_iota(jnp.int32, (LANES, LANES), 0)
    col = lax.broadcasted_iota(jnp.int32, (LANES, LANES), 1)
    head = jnp.where(col < 64, 2 * pair + 1, 2 * pair)
    spot = jnp.where(col < 64, col, col - 64)
    term = jnp.where(for_query, spot, spot - 3)
    is_term = (term >= 0) & (term < 3) & (row == term * local_heads + head)
    ones = jnp.where(for_query, spot - 3, spot)
    is_one = (ones >= 0) & (ones < 3) & (row == 3 * local_heads)
    sign = 1.0 if for_query else -1.0
    return (jnp.where(is_term, sign, 0.0) + jnp.where(is_one, 1.0, 0.0)).astype(bf16)


def allowed_pairs(start, first_key, query_tile, rows, begin_row):
    shape = (K_TILE, Q_TILE)
    key_place = first_key + lax.broadcasted_iota(jnp.int32, shape, 0)
    query_place = rows + query_tile * Q_TILE + lax.broadcasted_iota(jnp.int32, shape, 1)
    return (key_place >= begin_row) & (key_place <= query_place)


def key_loops(ranges_ref, query_tile, rows, step, carry):
    first = ranges_ref[0, query_tile]
    full = ranges_ref[1, query_tile]
    diagonal = (rows + query_tile * Q_TILE) // K_TILE
    full = jnp.minimum(full, diagonal)
    carry = lax.fori_loop(first, full, functools.partial(step, True), carry)
    carry = lax.fori_loop(full, diagonal, functools.partial(step, False), carry)
    return lax.fori_loop(
        diagonal, diagonal + Q_TILE // K_TILE, functools.partial(step, True), carry
    )


def fill_keys(pair, local_heads, sources, keys, chunk):
    place = placing(pair, local_heads, False)
    rows = sources[0][0].shape[0]
    lane = lax.broadcasted_iota(jnp.int32, (chunk, LANES), 1)
    for half, (key_ref, terms_ref) in enumerate(sources):

        def fill(n, carry):
            here = pl.ds(pl.multiple_of(n * chunk, chunk), chunk)
            there = pl.ds(pl.multiple_of(half * rows + n * chunk, chunk), chunk)
            extra = dot(terms_ref[here, :], place).astype(bf16)
            key = key_ref[here, :]
            keys[0][there, :] = jnp.where(lane < 64, key, extra)
            keys[1][there, :] = jnp.where(lane < 64, extra, key)
            return carry

        lax.fori_loop(0, rows // chunk, fill, 0)


def query_tiles(q_ref, terms_ref, place, here, scaling):
    lane = lax.broadcasted_iota(jnp.int32, (Q_TILE, LANES), 1)
    extra = dot(terms_ref[here, :], place).astype(bf16)
    query = (q_ref[here, :].astype(f32) * scaling).astype(bf16)
    return jnp.where(lane < 64, query, extra), jnp.where(lane < 64, extra, query)


def attend_kernel(
    local_heads,
    ranges_ref,
    q_ref,
    k_own_ref,
    v_own_ref,
    k_prev_ref,
    v_prev_ref,
    t_own_ref,
    t_prev_ref,
    begin_ref,
    o_ref,
    lse_ref,
    key0,
    key1,
    values,
    acc0,
    acc1,
):
    pair = pl.program_id(0)
    rows = q_ref.shape[0]
    chunk = 512
    keys, accs = (key0, key1), (acc0, acc1)
    fill_keys(
        pair, local_heads, ((k_prev_ref, t_prev_ref), (k_own_ref, t_own_ref)), keys, chunk
    )
    for half, v_ref in enumerate((v_prev_ref, v_own_ref)):
        for n in range(rows // chunk):
            values[:, half * rows + n * chunk : half * rows + (n + 1) * chunk] = v_ref[
                n * chunk : (n + 1) * chunk, :
            ].T
    place = placing(pair, local_heads, True)

    def query_loop(tile, carry):
        here = pl.ds(pl.multiple_of(tile * Q_TILE, Q_TILE), Q_TILE)
        queries = query_tiles(q_ref, t_own_ref, place, here, 64**-0.5)
        begin_row = begin_ref[0:1, here]
        for acc in accs:
            acc[...] = jnp.zeros_like(acc)

        def step(masked, number, state):
            first_key = pl.multiple_of(number * K_TILE, K_TILE)
            there = pl.ds(first_key, K_TILE)
            fresh = []
            if masked:
                allowed = allowed_pairs(None, first_key, tile, rows, begin_row)
            for h in range(2):
                largest, total = state[2 * h], state[2 * h + 1]
                scores = dot(keys[h][there, :], queries[h], NT)
                if masked:
                    scores = jnp.where(allowed, scores, FAR)
                now = jnp.maximum(largest, jnp.max(scores, axis=0, keepdims=True))
                fade = jnp.exp(largest - now)
                weights = jnp.exp(scores - now)
                total = total * fade + jnp.sum(weights, axis=0, keepdims=True)
                accs[h][...] = accs[h][...] * fade + dot(
                    values[64 * h : 64 * (h + 1), there], weights.astype(bf16)
                )
                fresh += [now, total]
            return tuple(fresh)

        low = jnp.full((1, Q_TILE), FAR, f32)
        zero = jnp.zeros((1, Q_TILE), f32)
        state = key_loops(ranges_ref, tile, rows, step, (low, zero, low, zero))
        mixed = jnp.concatenate(
            [accs[h][...] * (1.0 / state[2 * h + 1]) for h in range(2)], axis=0
        )
        o_ref[here, :] = mixed.T.astype(bf16)
        for h in range(2):
            lse_ref[h : h + 1, here] = state[2 * h] + jnp.log(state[2 * h + 1])
        return carry

    lax.fori_loop(0, rows // Q_TILE, query_loop, 0)


def lane_block(rows, offset):
    return pl.BlockSpec((rows, LANES), lambda p, *_: (0, offset + p))


def fixed(shape):
    return pl.BlockSpec(shape, lambda p, *_: (0, 0))


def attend(ranges, query, key_value, earlier, terms, earlier_terms, begins, local_heads):
    rows = query.shape[0]
    pairs = local_heads // 2
    return pl.pallas_call(
        functools.partial(attend_kernel, local_heads),
        grid_spec=pltpu.PrefetchScalarGridSpec(
            num_scalar_prefetch=1,
            grid=(pairs,),
            in_specs=[
                lane_block(rows, 0),
                lane_block(rows, 0),
                lane_block(rows, pairs),
                lane_block(rows, 0),
                lane_block(rows, pairs),
                fixed((rows, LANES)),
                fixed((rows, LANES)),
                fixed((8, rows)),
            ],
            out_specs=[lane_block(rows, 0), pl.BlockSpec((8, rows), lambda p, *_: (p, 0))],
            scratch_shapes=[
                pltpu.VMEM((2 * rows, LANES), bf16),
                pltpu.VMEM((2 * rows, LANES), bf16),
                pltpu.VMEM((LANES, 2 * rows), bf16),
                pltpu.VMEM((64, Q_TILE), f32),
                pltpu.VMEM((64, Q_TILE), f32),
            ],
        ),
        out_shape=(
            jax.ShapeDtypeStruct((rows, pairs * LANES), bf16),
            jax.ShapeDtypeStruct((8 * pairs, rows), f32),
        ),
        cost_estimate=pl.CostEstimate(
            flops=40_000_000_000, transcendentals=20_000_000, bytes_accessed=12_000_000
        ),
        name="attend",
    )(ranges, query, key_value, key_value, earlier, earlier, terms, earlier_terms, begins)


def attend_back_kernel(
    local_heads,
    ranges_ref,
    q_ref,
    k_own_ref,
    v_own_ref,
    k_prev_ref,
    v_prev_ref,
    t_own_ref,
    t_prev_ref,
    begin_ref,
    grad_ref,
    o_ref,
    lse_ref,
    dq_ref,
    dk_own_ref,
    dv_own_ref,
    dk_prev_ref,
    dv_prev_ref,
    decay_own_ref,
    decay_prev_ref,
    key0,
    key1,
    key_t0,
    key_t1,
    values,
    dk0,
    dk1,
    dv,
    dq0,
    dq1,
):
    pair = pl.program_id(0)
    rows = q_ref.shape[0]
    chunk = 512
    keys, keys_t, dks, dqs = (key0, key1), (key_t0, key_t1), (dk0, dk1), (dq0, dq1)
    fill_keys(
        pair, local_heads, ((k_prev_ref, t_prev_ref), (k_own_ref, t_own_ref)), keys, chunk
    )
    for n in range(2 * rows // chunk):
        part = slice(n * chunk, (n + 1) * chunk)
        for h in range(2):
            keys_t[h][:, part] = keys[h][part, :].T
    values[0:rows, :] = v_prev_ref[...]
    values[rows : 2 * rows, :] = v_own_ref[...]
    for ref in (dk0, dk1, dv):
        ref[...] = jnp.zeros_like(ref)
    place = placing(pair, local_heads, True)
    lane = lax.broadcasted_iota(jnp.int32, (Q_TILE, LANES), 1)
    pick_row = lax.broadcasted_iota(jnp.int32, (8, LANES), 0)
    pick_lane = lax.broadcasted_iota(jnp.int32, (8, LANES), 1)
    pick = jnp.where((pick_lane // 64) == pick_row, 1.0, 0.0)

    @pl.when(pair == 0)
    def _():
        decay_own_ref[...] = jnp.zeros_like(decay_own_ref)
        decay_prev_ref[...] = jnp.zeros_like(decay_prev_ref)

    def query_loop(tile, carry):
        here = pl.ds(pl.multiple_of(tile * Q_TILE, Q_TILE), Q_TILE)
        queries = query_tiles(q_ref, t_own_ref, place, here, 64**-0.5)
        begin_row = begin_ref[0:1, here]
        grad = grad_ref[here, :]
        nothing = jnp.zeros_like(grad)
        grads = (jnp.where(lane < 64, grad, nothing), jnp.where(lane < 64, nothing, grad))
        product = grad.astype(f32) * o_ref[here, :].astype(f32)
        inner = dot(pick, product, NT, precision=lax.Precision.HIGHEST)
        for dq in dqs:
            dq[...] = jnp.zeros_like(dq)

        def step(masked, number, state):
            first_key = pl.multiple_of(number * K_TILE, K_TILE)
            there = pl.ds(first_key, K_TILE)
            if masked:
                allowed = allowed_pairs(None, first_key, tile, rows, begin_row)
            value = values[there, :]
            value_part = 0.0
            for h in range(2):
                scores = dot(keys[h][there, :], queries[h], NT)
                prob = jnp.exp(scores - lse_ref[h : h + 1, here])
                if masked:
                    prob = jnp.where(allowed, prob, 0.0)
                grad_prob = dot(value, grads[h], NT)
                grad_score = (prob * (grad_prob - inner[h : h + 1, :])).astype(bf16)
                value_part = value_part + dot(prob.astype(bf16), grads[h])
                dks[h][there, :] += dot(grad_score, queries[h])
                dqs[h][...] += dot(keys_t[h][:, there], grad_score)
            dv[there, :] += value_part
            return state

        key_loops(ranges_ref, tile, rows, step, 0)
        turned = [dq[...].T for dq in dqs]
        dq_ref[here, :] = (jnp.where(lane < 64, turned[0], turned[1]) * 64**-0.5).astype(bf16)
        decay = decay_own_ref[here, :]
        decay = decay + jnp.where(lane == 2 * pair, turned[0][:, 64:65], 0.0)
        decay = decay + jnp.where(lane == 2 * pair + 1, turned[1][:, 0:1], 0.0)
        decay_own_ref[here, :] = decay
        return carry

    lax.fori_loop(0, rows // Q_TILE, query_loop, 0)

    def finish(n, carry):
        for half, dk_ref, dv_ref, decay_ref, sign in (
            (0, dk_prev_ref, dv_prev_ref, decay_prev_ref, 1.0),
            (1, dk_own_ref, dv_own_ref, decay_own_ref, -1.0),
        ):
            here = pl.ds(pl.multiple_of(n * chunk, chunk), chunk)
            there = pl.ds(pl.multiple_of(half * rows + n * chunk, chunk), chunk)
            first, second = dk0[there, :], dk1[there, :]
            dk_ref[here, :] = jnp.where(lane < 64, first, second).astype(dk_ref.dtype)
            dv_ref[here, :] = dv[there, :].astype(dv_ref.dtype)
            decay = decay_ref[here, :]
            decay = decay + jnp.where(lane == 2 * pair, sign * first[:, 67:68], 0.0)
            decay = decay + jnp.where(lane == 2 * pair + 1, sign * second[:, 3:4], 0.0)
            decay_ref[here, :] = decay
        return carry

    lax.fori_loop(0, rows // chunk, finish, 0)


def attend_back(
    ranges, query, key_value, earlier, terms, earlier_terms, begins, grad, mixed, lse, local_heads
):
    rows = query.shape[0]
    pairs = local_heads // 2
    wide = pairs * LANES
    return pl.pallas_call(
        functools.partial(attend_back_kernel, local_heads),
        grid_spec=pltpu.PrefetchScalarGridSpec(
            num_scalar_prefetch=1,
            grid=(pairs,),
            in_specs=[
                lane_block(rows, 0),
                lane_block(rows, 0),
                lane_block(rows, pairs),
                lane_block(rows, 0),
                lane_block(rows, pairs),
                fixed((rows, LANES)),
                fixed((rows, LANES)),
                fixed((8, rows)),
                lane_block(rows, 0),
                lane_block(rows, 0),
                pl.BlockSpec((8, rows), lambda p, *_: (p, 0)),
            ],
            out_specs=[lane_block(rows, 0)] * 5 + [fixed((rows, LANES))] * 2,
            scratch_shapes=[
                pltpu.VMEM((2 * rows, LANES), bf16),
                pltpu.VMEM((2 * rows, LANES), bf16),
                pltpu.VMEM((LANES, 2 * rows), bf16),
                pltpu.VMEM((LANES, 2 * rows), bf16),
                pltpu.VMEM((2 * rows, LANES), bf16),
                pltpu.VMEM((2 * rows, LANES), f32),
                pltpu.VMEM((2 * rows, LANES), f32),
                pltpu.VMEM((2 * rows, LANES), f32),
                pltpu.VMEM((LANES, Q_TILE), f32),
                pltpu.VMEM((LANES, Q_TILE), f32),
            ],
        ),
        out_shape=(
            jax.ShapeDtypeStruct((rows, wide), bf16),
            jax.ShapeDtypeStruct((rows, wide), f32),
            jax.ShapeDtypeStruct((rows, wide), f32),
            jax.ShapeDtypeStruct((rows, wide), bf16),
            jax.ShapeDtypeStruct((rows, wide), bf16),
            jax.ShapeDtypeStruct((rows, LANES), f32),
            jax.ShapeDtypeStruct((rows, LANES), f32),
        ),
        cost_estimate=pl.CostEstimate(
            flops=80_000_000_000, transcendentals=20_000_000, bytes_accessed=25_000_000
        ),
        name="attend_back",
    )(
        ranges, query, key_value, key_value, earlier, earlier, terms, earlier_terms, begins,
        grad, mixed, lse,
    )


def normalize(hidden):
    factor = lax.rsqrt(jnp.mean(hidden * hidden, axis=1, keepdims=True) + epsilon)
    return (hidden * factor, factor)


def norm_back(grad_hat, normed, factor):
    return factor * (grad_hat - normed * jnp.mean(grad_hat * normed, axis=1, keepdims=True))


def over_tokens(operand, other_side):
    return lax.dot_general(
        operand, other_side, (((0,), (0,)), ((), ())), preferred_element_type=f32
    )


def gathered(pieces, groups):
    packed = jnp.concatenate(
        [piece.reshape(piece.shape[0], groups, -1) for piece in pieces], axis=2
    )
    mine = lax.all_to_all(packed, "head", split_axis=1, concat_axis=0, tiled=True)
    mine = mine.reshape(mine.shape[0], mine.shape[2])
    return lax.all_gather(mine, "blk", axis=0, tiled=True)


def scattered(grad, groups):
    summed = lax.psum_scatter(grad, "blk", scatter_dimension=0, tiled=True)
    rows, columns = summed.shape
    parts = lax.all_to_all(
        summed.reshape(groups, rows // groups, columns), "head", split_axis=0, concat_axis=0
    )
    return jnp.swapaxes(parts, 0, 1).astype(f32)


def body(
    tokens,
    segment,
    norm1_gain,
    w_query,
    w_key,
    w_value,
    w_gate_out,
    w_forget,
    forget_bias,
    w_output,
    norm2_gain,
    w_gate,
    w_up,
    w_down,
    cotangent,
):
    token_rows, model_width = tokens.shape
    groups = lax.axis_size("head")
    head_count = forget_bias.shape[0]
    local_heads = head_count // groups
    local_width = model_width // groups
    hidden_width = w_gate.shape[1] // groups
    rows = token_rows * groups
    share = w_query.shape[0]
    group = lax.axis_index("head")

    low = lambda array: array.astype(bf16)
    spread = lambda gain: jnp.broadcast_to(low(gain)[:, None, None], (share, groups, 1))
    forget_low = low(w_forget).reshape(share, groups, local_heads)
    rest = LANES - local_heads - 2
    small = jnp.concatenate(
        [forget_low, spread(norm1_gain), spread(norm2_gain), jnp.zeros((share, groups, rest), bf16)],
        axis=2,
    )
    first = gathered([low(w_key), low(w_value), low(w_query), low(w_gate_out), small], groups)
    tokens_all = lax.all_gather(tokens, "head", axis=0, tiled=True)
    output_weight = gathered([low(w_output)], groups)
    second = gathered([low(w_gate), low(w_up), low(w_down)], groups)
    cotangent_all = lax.all_gather(cotangent, "head", axis=0, tiled=True)

    segment_plus = segment + 1
    earlier_segment = passed_along(segment_plus, "blk", 1)
    window = jnp.concatenate([earlier_segment, segment_plus])
    begins = jnp.sum(
        (window[:, None] < segment_plus[None, :]).astype(jnp.int32), axis=0
    )
    tiles = begins.reshape(rows // Q_TILE, Q_TILE)
    ranges = jnp.stack([tiles[:, 0] // K_TILE, (tiles[:, -1] + K_TILE - 1) // K_TILE])
    begins = jnp.broadcast_to(begins[None, :], (8, rows))

    gain1 = first[:, 4 * local_width + local_heads].astype(f32)
    gain2 = first[:, 4 * local_width + local_heads + 1].astype(f32)
    normed_all, _ = normalize(tokens_all.astype(f32))
    input1 = (normed_all * gain1).astype(bf16)
    key_value = dot(input1, first[:, : 2 * local_width]).astype(bf16)
    earlier_kv = passed_along(key_value, "blk", 1)
    query = dot(input1, first[:, 2 * local_width : 3 * local_width]).astype(bf16)
    gate_forget = dot(input1, first[:, 3 * local_width :])
    gate_raw = gate_forget[:, :local_width]
    bias = lax.dynamic_slice_in_dim(forget_bias, group * local_heads, local_heads, 0)
    bias = jnp.pad(bias, (0, LANES - local_heads))
    forget = (gate_forget[:, local_width:] + bias[None, :]).astype(bf16).astype(f32)
    terms, halo_terms = decay_terms(jax.nn.log_sigmoid(forget), local_heads)
    earlier_terms = passed_along(halo_terms, "blk", 1)

    attended, lse = attend(
        ranges, query, key_value, earlier_kv, terms, earlier_terms, begins, local_heads
    )
    opened = jax.nn.sigmoid(gate_raw)
    attended_wide = attended.astype(f32)
    gated = (opened * attended_wide).astype(bf16)
    branch = dot(gated, output_weight, NT).astype(bf16)
    inputs = tokens.astype(f32)
    middle = inputs + lax.psum_scatter(branch, "head", scatter_dimension=0, tiled=True).astype(f32)
    normed2, factor2 = normalize(middle)
    input2 = lax.all_gather(
        (normed2 * gain2).astype(bf16), "head", axis=0, tiled=True
    )
    gate_act = dot(input2, second[:, :hidden_width])
    up_act = dot(input2, second[:, hidden_width : 2 * hidden_width])
    opening = jax.nn.sigmoid(gate_act)
    hidden = (gate_act * opening * up_act).astype(bf16)
    down = dot(hidden, second[:, 2 * hidden_width :], NT).astype(bf16)
    grad_hidden = dot(cotangent_all, second[:, 2 * hidden_width :])
    grad_gate_act = (grad_hidden * up_act * opening * (1.0 + gate_act * (1.0 - opening))).astype(
        bf16
    )
    grad_up_act = (grad_hidden * gate_act * opening).astype(bf16)
    grad_act = jnp.concatenate([grad_gate_act, grad_up_act], axis=1)
    grad_input2 = dot(grad_act, second[:, : 2 * hidden_width], NT).astype(bf16)
    grad_input2 = lax.psum_scatter(
        grad_input2, "head", scatter_dimension=0, tiled=True
    ).astype(f32)
    grad_middle = cotangent.astype(f32) + norm_back(grad_input2 * gain2, normed2, factor2)
    grad_branch = lax.all_gather(grad_middle.astype(bf16), "head", axis=0, tiled=True)
    result = (
        middle + lax.psum_scatter(down, "head", scatter_dimension=0, tiled=True).astype(f32)
    ).astype(bf16)
    second_grad = jnp.concatenate(
        [over_tokens(input2, grad_act).astype(bf16), over_tokens(cotangent_all, hidden).astype(bf16)],
        axis=1,
    )
    second_sum = scattered(second_grad, groups)

    grad_gated = dot(grad_branch, output_weight)
    grad_attended = (grad_gated * opened).astype(bf16)
    grad_gate_pre = (grad_gated * attended_wide * opened * (1.0 - opened)).astype(bf16)
    output_sum = scattered(over_tokens(grad_branch, gated).astype(bf16), groups)

    dq, dk_own, dv_own, dk_prev, dv_prev, decay_own, decay_prev = attend_back(
        ranges, query, key_value, earlier_kv, terms, earlier_terms, begins,
        grad_attended, attended, lse, local_heads,
    )
    dk = (dk_own + passed_along(dk_prev, "blk", -1).astype(f32)).astype(bf16)
    dv = (dv_own + passed_along(dv_prev, "blk", -1).astype(f32)).astype(bf16)
    decay_later = passed_along(decay_prev, "blk", -1)
    logf_grad = decay_back(decay_own, decay_later)
    forget_grad = jnp.where(
        jnp.arange(LANES)[None, :] < local_heads, logf_grad * jax.nn.sigmoid(-forget), 0.0
    ).astype(bf16)
    grads = jnp.concatenate([dk, dv, dq, grad_gate_pre, forget_grad], axis=1)
    grad_input1 = dot(grads, first, NT).astype(bf16)
    grad_input1 = lax.psum_scatter(
        grad_input1, "head", scatter_dimension=0, tiled=True
    ).astype(f32)
    normed1, factor1 = normalize(inputs)
    tokens_grad = grad_middle + norm_back(grad_input1 * gain1, normed1, factor1)

    first_grad = over_tokens(input1, grads)
    bias_part = jnp.sum(forget_grad.astype(f32), axis=0)
    row = jnp.arange(model_width)[:, None] % share
    column = jnp.arange(4 * local_width + LANES)[None, :]
    spread_bias = jnp.sum(
        jnp.where(row[:, :, None] == jnp.arange(local_heads)[None, None, :], bias_part[:local_heads], 0.0),
        axis=2,
    )
    first_grad = jnp.where(
        column == 4 * local_width + local_heads, spread_bias, first_grad
    ).astype(bf16)
    first_sum = scattered(first_grad, groups)

    def columns(array, start, width):
        return array[:, :, start : start + width].reshape(share, groups * width)

    key_sum, value_sum, query_sum, gate_out_sum = (
        columns(first_sum, n * local_width, local_width) for n in range(4)
    )
    forget_sum = columns(first_sum, 4 * local_width, local_heads)
    bias_total = first_sum[:local_heads, :, 4 * local_width + local_heads].T.reshape(head_count)
    gate_sum, up_sum, down_sum = (
        columns(second_sum, n * hidden_width, hidden_width) for n in range(3)
    )
    output_total = columns(output_sum, 0, local_width)

    def along(weight, grad):
        return jnp.sum(low(weight).astype(f32) * grad, axis=1)

    gain1_total = (
        along(w_query, query_sum)
        + along(w_key, key_sum)
        + along(w_value, value_sum)
        + along(w_gate_out, gate_out_sum)
        + along(w_forget, forget_sum)
    ) / low(norm1_gain).astype(f32)
    gain2_total = (along(w_gate, gate_sum) + along(w_up, up_sum)) / low(norm2_gain).astype(f32)
    return (
        result,
        tokens_grad,
        gain1_total,
        query_sum,
        key_sum,
        value_sum,
        gate_out_sum,
        forget_sum,
        bias_total,
        output_total,
        gain2_total,
        gate_sum,
        up_sum,
        down_sum,
    )


def solution(mesh):
    both = ("blk", "head")
    matrix, vector = P(both, None), P(both)
    return jax.shard_map(
        body,
        mesh=mesh,
        in_specs=(
            matrix, P("blk"), vector, matrix, matrix, matrix, matrix, matrix, P(), matrix, vector,
            matrix, matrix, matrix, matrix,
        ),
        out_specs=(
            matrix, matrix, vector, matrix, matrix, matrix, matrix, matrix, P(), matrix, vector,
            matrix, matrix, matrix,
        ),
        check_vma=False,
    )
```

time: 2840 us -> 1380 us (0.49)
  waiting for transfers between devices: 1510 us -> 899 us
  matrix products: 651 us -> 181 us
  blocking collectives: 219 us -> 33.4 us
  other arithmetic: 227 us -> 57.7 us
  Pallas kernels: 0 us -> 135 us
  local copies, waits for them, and re-layouts: 153 us -> 20.7 us
    reduce_scatter x7, waiting for transfers between devices: 929 us -> 377 us  [the longest x3 160 us: scattered(): summed = lax.psum_scatter(grad, 'blk', scatter_dimension=0, tiled=True)]
    dot_general x46 -> x11, matrix products: 573 us -> 131 us  [dot(): return lax.dot_general(a, b, dims, preferred_element_type=f32, **kw)]
    unnamed x19 -> x14, waiting for transfers between devices: 253 us -> 1.43 us
    all_gather x8 -> x7, waiting for transfers between devices: 147 us -> 354 us  [the longest x3 217 us: gathered(): return lax.all_gather(mine, 'blk', axis=0, tiled=True)]
    reduce_sum x9 -> x11, other arithmetic: 170 us -> 14.6 us  [the longest x7 7.17 us: along(): return jnp.sum(low(weight).astype(f32) * grad, axis=1)]
    pallas_call x0 -> x4, Pallas kernels: none -> 135 us  [the longest x1 73.3 us: attend_back(): pl.pallas_call(functools.partial(attend_back_kernel, local_heads), grid_s...]
    unnamed x152 -> x101, local copies, waits for them, and re-layouts: 81.8 us -> 8 us
    psum x1 -> x0, blocking collectives: 53.1 us -> none  [body(): lax.psum((grad_first_gain, grad_second_gain, bias_local), ('blk', 'head'))]
  transfers between devices with their start and end apart: 30 -> 24, of which waited for: 17 -> 20; matrix products, arithmetic and copies ran while one was open for 18% -> 13% of each run, Pallas kernels for 0% -> 10%
where the time goes in v1:
time: 1380 us; the launch traced here: 1370 us
  waiting for transfers between devices  899 us (65%)
  matrix products  181 us (13%)
  Pallas kernels  135 us (10%)
  other arithmetic  57.7 us (4%)
  blocking collectives  33.4 us (2%)
  starting transfers between devices  30.5 us (2%)
  local copies, waits for them, and re-layouts  20.7 us (2%)
  between operations  15.2 us (1%)
    all_gather x3, waiting for transfers between devices, gathered(): return lax.all_gather(mine, 'blk', axis=0, tiled=True)  217 us
    reduce_scatter x3, waiting for transfers between devices, scattered(): summed = lax.psum_scatter(grad, 'blk', scatter_dimension=0, tiled=True)  160 us
    ppermute x6, waiting for transfers between devices, passed_along(): return lax.ppermute(array, axis, pairs)  140 us
    dot_general x11, matrix products, dot(): return lax.dot_general(a, b, dims, preferred_element_type=f32, **kw)  131 us
    pallas_call x1, Pallas kernels, attend_back(): pl.pallas_call(functools.partial(attend_back_kernel, local_heads), grid_s...  73.3 us
    reduce_scatter x1, waiting for transfers between devices, body(): lax.psum_scatter(branch, 'head', scatter_dimension=0, tiled=True)  65.1 us
    reduce_scatter x1, waiting for transfers between devices, body(): lax.psum_scatter(down, 'head', scatter_dimension=0, tiled=True).astype(f32)  58.8 us
    reduce_scatter x1, waiting for transfers between devices, body(): lax.psum_scatter(grad_input2, 'head', scatter_dimension=0, tiled=True)  58.1 us
  transfers between devices with their start and end apart: 24, of which 20 were waited for; matrix products, arithmetic and copies ran while one was open for 13% of the time, Pallas kernels for 10%

profile of v1, /device:TPU:0, one launch (start us, length us, event | category | flops | bytes accessed | tf_op | source)
XLA Modules:
  0.0 1372.9 jit_solution(17577688206958866122)
XLA Ops:
  14.7 14.2 %all_to_all.60 = bf16[48,4,1664]{2,0,1:T(8,128)(2,1)} all-to-all(bf16[48,4,1664]{2,0,1:T(8,128)(2,1)S(1)} %copy.103), channel_id=1, replica_groups=mesh['blk'=8,'head'=4] {'head'}, dimensions={1} | all-to-all | bytes 1277952 | tf_op jit(solution)/shard_map/all_to_all | solution.py:480
  37.7 76.7 %all-gather.10.cloned.1.call-done = bf16[1536,1664]{1,0:T(8,128)(2,1)} async-done(((bf16[192,1664]{1,0:T(8,128)(2,1)}), bf16[1536,1664]{1,0:T(8,128)(2,1)}) %all-gather.10.cloned.1.call-update) | async-done | bytes 5111824 | tf_op jit(solution)/shard_map/all_gather | solution.py:482
  116.3 44.3 %all-gather.8.cloned.1.call-done = bf16[2048,1536]{1,0:T(8,128)(2,1)} async-done(((bf16[512,1536]{1,0:T(8,128)(2,1)}), bf16[2048,1536]{1,0:T(8,128)(2,1)}) %all-gather.8.cloned.1.call-update) | async-done | bytes 6291472 | tf_op jit(solution)/shard_map/all_gather | solution.py:530
  206.7 57.3 %collective-permute-done.2.t_prev_ref = bf16[2048,128]{1,0:T(8,128)(2,1)S(1)} collective-permute-done((bf16[2048,128]{1,0:T(8,128)(2,1)}, bf16[2048,128]{1,0:T(8,128)(2,1)S(1)}, u32[]{:S(2)}, u32[]{:S(2)}) %collective-permute-start.2) | collective-permute-done | bytes 524320 | tf_op jit(solution)/shard_map/ppermute | solution.py:28
  264.8 53.8 %attend.1 = (bf16[2048,384]{1,0:T(8,128)(2,1)}, f32[24,2048]{1,0:T(8,128)}) custom-call(s32[2,4]{1,0:T(2,128)} %pad_add_fusion.1.ranges_ref, bf16[2048,384]{1,0:T(8,128)(2,1)} %convolution_convert_fusion.8.q_ref, bf16[2048,768]{1,0:T(8,128)(2,1)} %convolution_convert_fusion.6.k_own_ref.v_own_ref, ...), custom_call_target="tpu_custom_call" | custom-call | flops 40000000000 | bytes 12000000 | tf_op jit(solution)/shard_map/attend/pallas_call | solution.py:249
  330.4 19.2 %all_to_all.61 = bf16[48,4,3072]{2,0,1:T(8,128)(2,1)} all-to-all(bf16[48,4,3072]{2,0,1:T(8,128)(2,1)S(1)} %copy.105), channel_id=1, replica_groups=mesh['blk'=8,'head'=4] {'head'}, dimensions={1} | all-to-all | bytes 2359296 | tf_op jit(solution)/shard_map/all_to_all | solution.py:480
  349.9 65.1 %reduce-scatter.8.cloned.1.call-done = bf16[512,1536]{1,0:T(8,128)(2,1)} async-done(((bf16[2048,1536]{1,0:T(8,128)(2,1)}), bf16[512,1536]{1,0:T(8,128)(2,1)}) %reduce-scatter.8.cloned.1.call-update) | async-done | bytes 1572880 | tf_op jit(solution)/shard_map/reduce_scatter | solution.py:568
  419.0 43.9 %all-gather.18.cloned.1.call-done = bf16[2048,1536]{1,0:T(8,128)(2,1)} async-done(((bf16[512,1536]{1,0:T(8,128)(2,1)}), bf16[2048,1536]{1,0:T(8,128)(2,1)}) %all-gather.18.cloned.1.call-update) | async-done | bytes 6291472 | tf_op jit(solution)/shard_map/all_gather | solution.py:533
  462.9 140.4 %all-gather.16.cloned.1.call-done = bf16[1536,3072]{1,0:T(8,128)(2,1)} async-done(((bf16[192,3072]{1,0:T(8,128)(2,1)}), bf16[1536,3072]{1,0:T(8,128)(2,1)}) %all-gather.16.cloned.1.call-update) | async-done | bytes 9437200 | tf_op jit(solution)/shard_map/all_gather | solution.py:482
  603.3 11.8 fusion.29
  615.1 34.5 %all-gather.14.cloned.1.call-done = bf16[2048,1536]{1,0:T(8,128)(2,1)} async-done(((bf16[512,1536]{1,0:T(8,128)(2,1)}), bf16[2048,1536]{1,0:T(8,128)(2,1)}) %all-gather.14.cloned.1.call-update) | async-done | bytes 6291472 | tf_op jit(solution)/shard_map/all_gather | solution.py:570
  649.5 11.8 fusion.23
  661.3 19.9 %fusion.5 = (bf16[2048,1024]{0,1:T(8,128)(2,1)}, bf16[2048,1024]{0,1:T(8,128)(2,1)}, bf16[2048,1024]{0,1:T(8,128)(2,1)}) fusion(f32[1024,2048]{1,0:T(8,128)} %fusion.29, f32[2048,1024]{0,1:T(8,128)} %fusion.23, bf16[2048,1536]{1,0:T(8,128)(2,1)} %all-gather.14.cloned.1.call-done, bf16[1536,3072]{1,0:T(8,128)(2,1)} %all-gather.16.cloned.1.call-done), kind=kOutput, calls=%fused_computation.13 | convolution fusion | flops 6476005376 | bytes 38797312 | tf_op jit(solution)/shard_map/dot_general | solution.py:22
  681.3 19.1 %convolution_convert_fusion.4 = bf16[2048,1536]{1,0:T(8,128)(2,1)} fusion(bf16[1536,3072]{1,0:T(8,128)(2,1)} %all-gather.16.cloned.1.call-done, bf16[2048,1024]{0,1:T(8,128)(2,1)} %get-tuple-element.45, bf16[2048,1024]{0,1:T(8,128)(2,1)} %get-tuple-element.44), kind=kOutput, calls=%fused_computation.22 | convolution fusion | flops 12904824832 | bytes 20971520 | tf_op jit(solution)/shard_map/dot_general | solution.py:22
  700.9 58.1 %reduce-scatter.12.cloned.1.call-done = bf16[512,1536]{1,0:T(8,128)(2,1)} async-done(((bf16[2048,1536]{1,0:T(8,128)(2,1)}), bf16[512,1536]{1,0:T(8,128)(2,1)}) %reduce-scatter.12.cloned.1.call-update) | async-done | bytes 1572880 | tf_op jit(solution)/shard_map/reduce_scatter | solution.py:585
  765.3 10.3 fusion.11
  775.6 16.8 %convolution_convert_fusion.2 = bf16[1536,2048]{1,0:T(8,128)(2,1)S(1)} fusion(bf16[2048,1536]{1,0:T(8,128)(2,1)} %all-gather.14.cloned.1.call-done, bf16[2048,1024]{0,1:T(8,128)(2,1)} %get-tuple-element.45, bf16[2048,1024]{0,1:T(8,128)(2,1)S(1)} %copy-done.46), kind=kOutput, calls=%fused_computation.20 | convolution fusion | flops 12904824832 | bytes 20971520 | tf_op jit(solution)/shard_map/dot_general | solution.py:471
  797.3 14.5 %all-gather.20.cloned.1.call-done = bf16[2048,1536]{1,0:T(8,128)(2,1)} async-done(((bf16[512,1536]{1,0:T(8,128)(2,1)}), bf16[2048,1536]{1,0:T(8,128)(2,1)}) %all-gather.20.cloned.1.call-update) | async-done | bytes 6291472 | tf_op jit(solution)/shard_map/all_gather | solution.py:589
  811.8 9.4 multiply_convert_fusion.1
  821.2 73.3 %attend_back.1 = (bf16[2048,384]{1,0:T(8,128)(2,1)}, f32[2048,384]{1,0:T(8,128)}, f32[2048,384]{1,0:T(8,128)}, bf16[2048,384]{1,0:T(8,128)(2,1)}, bf16[2048,384]...) custom-call(s32[2,4]{1,0:T(2,128)} %pad_add_fusion.1.ranges_ref, ...), custom_call_target="tpu_custom_call" | custom-call | flops 80000000000 | bytes 25000000 | tf_op jit(solution)/shard_map/attend_back/pallas_call | solution.py:410
  907.1 24.0 %collective-permute-done.5.halo_ref = f32[2048,128]{1,0:T(8,128)} collective-permute-done((f32[2048,128]{1,0:T(8,128)}, f32[2048,128]{1,0:T(8,128)}, u32[]{:S(2)}, u32[]{:S(2)}) %collective-permute-start.5) | collective-permute-done | bytes 1048608 | tf_op jit(solution)/shard_map/ppermute | solution.py:28
  937.5 27.4 %collective-permute-done.3 = bf16[2048,384]{1,0:T(8,128)(2,1)} collective-permute-done((bf16[2048,384]{1,0:T(8,128)(2,1)}, bf16[2048,384]{1,0:T(8,128)(2,1)}, u32[]{:S(2)}, u32[]{:S(2)}) %collective-permute-start.3) | collective-permute-done | bytes 1572896 | tf_op jit(solution)/shard_map/ppermute | solution.py:28
  966.8 31.6 %collective-permute-done.4 = bf16[2048,384]{1,0:T(8,128)(2,1)} collective-permute-done((bf16[2048,384]{1,0:T(8,128)(2,1)}, bf16[2048,384]{1,0:T(8,128)(2,1)}, u32[]{:S(2)}, u32[]{:S(2)}) %collective-permute-start.4) | collective-permute-done | bytes 1572896 | tf_op jit(solution)/shard_map/ppermute | solution.py:28
  1005.2 14.7 %select_convert_fusion = bf16[1536,1664]{1,0:T(8,128)(2,1)} fusion(bf16[2048,1664]{1,0:T(8,128)(2,1)S(1)} %constant_dynamic-update-slice_fusion, bf16[1536]{0:T(1024)(128)(2,1)S(1)} %fusion.52, pred[1664]{0:T(1024)(128)(4,1)S(1)} %iota_compare_fusion, bf16[2048,1536]{1,0:T(8,128)(2,1)S(1)} %bitcast.103, f32[1536]{0:T(1024)S(1)} %copy-done.29, ...), kind=kOutput, calls=%fused_computation.6 | convolution fusion | flops 10484121600 | bytes 18238080 | tf_op jit(solution)/shard_map/dot_general | solution.py:471
  1020.2 16.9 %convolution_convert_fusion.3 = bf16[2048,1536]{1,0:T(8,128)(2,1)} fusion(bf16[2048,1664]{1,0:T(8,128)(2,1)} %copy-done.24, bf16[1536,1664]{1,0:T(8,128)(2,1)} %all-gather.10.cloned.1.call-done), kind=kOutput, calls=%fused_computation.21 | convolution fusion | flops 10472128512 | bytes 18219008 | tf_op jit(solution)/shard_map/dot_general | solution.py:22
  1037.2 11.6 convolution_convert_fusion
  1048.8 19.1 %reduce-scatter.20.cloned.1.call-done = bf16[192,3072]{1,0:T(8,128)(2,1)} async-done(((bf16[1536,3072]{1,0:T(8,128)(2,1)}), bf16[192,3072]{1,0:T(8,128)(2,1)}) %reduce-scatter.20.cloned.1.call-update) | async-done | bytes 1179664 | tf_op jit(solution)/shard_map/reduce_scatter | solution.py:486
  1072.1 15.2 %all-to-all-done.5 = bf16[4,48,3072]{2,1,0:T(8,128)(2,1)S(1)} async-done(((bf16[4,48,3072]{2,1,0:T(8,128)(2,1)}), bf16[4,48,3072]{2,1,0:T(8,128)(2,1)S(1)}, u32[]{:S(2)}, u32[]{:S(2)}) %all-to-all-start.5) | async-done | bytes 1179680 | tf_op jit(solution)/shard_map/all_to_all | solution.py:488
  1088.9 46.2 %reduce-scatter.18.cloned.1.call-done = bf16[192,384]{1,0:T(8,128)(2,1)} async-done(((bf16[1536,384]{1,0:T(8,128)(2,1)}), bf16[192,384]{1,0:T(8,128)(2,1)}) %reduce-scatter.18.cloned.1.call-update) | async-done | bytes 147472 | tf_op jit(solution)/shard_map/reduce_scatter | solution.py:486
  1143.3 95.0 %reduce-scatter.16.cloned.1.call-done = bf16[192,1664]{1,0:T(8,128)(2,1)} async-done(((bf16[1536,1664]{1,0:T(8,128)(2,1)}), bf16[192,1664]{1,0:T(8,128)(2,1)}) %reduce-scatter.16.cloned.1.call-update) | async-done | bytes 638992 | tf_op jit(solution)/shard_map/reduce_scatter | solution.py:486
  1264.7 34.2 %reduce-scatter.14.cloned.1.call-done = bf16[512,1536]{1,0:T(8,128)(2,1)} async-done(((bf16[2048,1536]{1,0:T(8,128)(2,1)}), bf16[512,1536]{1,0:T(8,128)(2,1)}) %reduce-scatter.14.cloned.1.call-update) | async-done | bytes 1572880 | tf_op jit(solution)/shard_map/reduce_scatter | solution.py:617
  1301.1 58.8 %reduce-scatter.10.cloned.1.call-done = bf16[512,1536]{1,0:T(8,128)(2,1)} async-done(((bf16[2048,1536]{1,0:T(8,128)(2,1)}), bf16[512,1536]{1,0:T(8,128)(2,1)}) %reduce-scatter.10.cloned.1.call-update) | async-done | bytes 1572880 | tf_op jit(solution)/shard_map/reduce_scatter | solution.py:591
  (240 shorter events, 168.6 us)
Async XLA Ops:
  7.2 107.3 %all-gather.10.cloned.1.call-start = ((), (), s32[]{:S(2)}) async-start(), calls=%async_computation.14 | async-start | bytes 5750784 | tf_op jit(solution)/shard_map/all_gather | solution.py:482
  28.9 131.7 %all-gather.8.cloned.1.call-start = ((), (), s32[]{:S(2)}) async-start(), calls=%async_computation.13 | async-start | bytes 7864320 | tf_op jit(solution)/shard_map/all_gather | solution.py:530
  29.7 8.0 collective-permute-start
  34.2 148.3 %all-to-all-start.1 = ((bf16[48,4,384]{2,0,1:T(8,128)(2,1)}), bf16[48,4,384]{2,0,1:T(8,128)(2,1)S(1)}, u32[]{:S(2)}, u32[]{:S(2)}) async-start(bf16[48,4,384]{2,0,1:T(8,128)(2,1)} %bitcast.100), calls=%async_computation.1 | async-start | bytes 294912 | tf_op jit(solution)/shard_map/all_to_all | solution.py:480
  37.6 281.0 %all-gather.12.cloned.1.call-start = ((), (), s32[]{:S(2)}) async-start(), calls=%async_computation.15 | async-start | bytes 1327104 | tf_op jit(solution)/shard_map/all_gather | solution.py:482
  37.7 152.1 %copy-start.40 = (f32[128]{0:T(128)}, f32[128]{0:T(128)S(1)}, u32[]{:S(2)}) copy-start(f32[128]{0:T(128)S(1)} %pad.4) | copy-start | bytes 1540
  116.3 645.9 %copy-start.26 = (f32[1536]{0:T(1024)}, f32[1536]{0:T(1024)S(1)}, u32[]{:S(2)}) copy-start(f32[1536]{0:T(1024)S(1)} %get-tuple-element.36) | copy-start | bytes 18436
  173.4 90.6 %collective-permute-start.1 = (bf16[2048,768]{1,0:T(8,128)(2,1)}, bf16[2048,768]{1,0:T(8,128)(2,1)}, u32[]{:S(2)}, u32[]{:S(2)}) collective-permute-start(bf16[2048,768]{1,0:T(8,128)(2,1)} %convolution_convert_fusion.6.k_own_ref.v_own_ref), channel_id=1, source_target_pairs={{0,4},{4,8},{8,12},{12,16},{16,20},{20,24},{24,28},{1,5},{5,9},{9,... | collective-permute-start | bytes 9437192 | tf_op jit(solution)/shard_map/ppermute | solution.py:28
  183.2 231.8 %reduce-scatter.8.cloned.1.call-start = ((), (), s32[]{:S(2)}) async-start(), calls=%async_computation.16 | async-start | bytes 7864320 | tf_op jit(solution)/shard_map/reduce_scatter | solution.py:568
  197.2 66.8 %collective-permute-start.2 = (bf16[2048,128]{1,0:T(8,128)(2,1)}, bf16[2048,128]{1,0:T(8,128)(2,1)S(1)}, u32[]{:S(2)}, u32[]{:S(2)}) collective-permute-start(bf16[2048,128]{1,0:T(8,128)(2,1)} %get-tuple-element.26), channel_id=1, source_target_pairs={{0,4},{4,8},{8,12},{12,16},{16,20},{20,24},{24,28},{1,5},{5,9},{9,... | collective-permute-start | bytes 1572872 | tf_op jit(solution)/shard_map/ppermute | solution.py:28
  327.5 135.5 %all-gather.18.cloned.1.call-start = ((), (), s32[]{:S(2)}) async-start(), calls=%async_computation.20 | async-start | bytes 7864320 | tf_op jit(solution)/shard_map/all_gather | solution.py:533
  328.0 275.2 %all-gather.16.cloned.1.call-start = ((), (), s32[]{:S(2)}) async-start(), calls=%async_computation.18 | async-start | bytes 10616832 | tf_op jit(solution)/shard_map/all_gather | solution.py:482
  349.6 299.9 %all-gather.14.cloned.1.call-start = ((), (), s32[]{:S(2)}) async-start(), calls=%async_computation.17 | async-start | bytes 7864320 | tf_op jit(solution)/shard_map/all_gather | solution.py:570
  417.1 345.1 %copy-start.30 = (f32[512]{0:T(512)}, f32[512]{0:T(512)S(1)}, u32[]{:S(2)}) copy-start(f32[512]{0:T(512)S(1)} %add_rsqrt_fusion.2) | copy-start | bytes 6148
  418.9 340.0 %reduce-scatter.12.cloned.1.call-start = ((), (), s32[]{:S(2)}) async-start(), calls=%async_computation.21 | async-start | bytes 7864320 | tf_op jit(solution)/shard_map/reduce_scatter | solution.py:585
  700.4 111.4 %all-gather.20.cloned.1.call-start = ((), (), s32[]{:S(2)}) async-start(), calls=%async_computation.22 | async-start | bytes 7864320 | tf_op jit(solution)/shard_map/all_gather | solution.py:589
  765.2 302.7 %reduce-scatter.20.cloned.1.call-start = ((), (), s32[]{:S(2)}) async-start(), calls=%async_computation.26 | async-start | bytes 10616832 | tf_op jit(solution)/shard_map/reduce_scatter | solution.py:486
  797.0 338.0 %reduce-scatter.18.cloned.1.call-start = ((), (), s32[]{:S(2)}) async-start(), calls=%async_computation.25 | async-start | bytes 1327104 | tf_op jit(solution)/shard_map/reduce_scatter | solution.py:486
  894.5 36.7 %collective-permute-start.5 = (f32[2048,128]{1,0:T(8,128)}, f32[2048,128]{1,0:T(8,128)}, u32[]{:S(2)}, u32[]{:S(2)}) collective-permute-start(f32[2048,128]{1,0:T(8,128)} %get-tuple-element.35), channel_id=1, source_target_pairs={{4,0},{8,4},{12,8},{16,12},{20,16},{24,20},{28,24},{5,1},{9,5},{13... | collective-permute-start | bytes 3145736 | tf_op jit(solution)/shard_map/ppermute | solution.py:28
  895.8 69.1 %collective-permute-start.3 = (bf16[2048,384]{1,0:T(8,128)(2,1)}, bf16[2048,384]{1,0:T(8,128)(2,1)}, u32[]{:S(2)}, u32[]{:S(2)}) collective-permute-start(bf16[2048,384]{1,0:T(8,128)(2,1)} %get-tuple-element.30), channel_id=1, source_target_pairs={{4,0},{8,4},{12,8},{16,12},{20,16},{24,20},{28,24},{5,1},{9,5},{13... | collective-permute-start | bytes 4718600 | tf_op jit(solution)/shard_map/ppermute | solution.py:28
  897.1 101.3 %collective-permute-start.4 = (bf16[2048,384]{1,0:T(8,128)(2,1)}, bf16[2048,384]{1,0:T(8,128)(2,1)}, u32[]{:S(2)}, u32[]{:S(2)}) collective-permute-start(bf16[2048,384]{1,0:T(8,128)(2,1)} %get-tuple-element.32), channel_id=1, source_target_pairs={{4,0},{8,4},{12,8},{16,12},{20,16},{24,20},{28,24},{5,1},{9,5},{13... | collective-permute-start | bytes 4718600 | tf_op jit(solution)/shard_map/ppermute | solution.py:28
  906.9 331.4 %reduce-scatter.16.cloned.1.call-start = ((), (), s32[]{:S(2)}) async-start(), calls=%async_computation.24 | async-start | bytes 5750784 | tf_op jit(solution)/shard_map/reduce_scatter | solution.py:486
  1019.9 279.0 %reduce-scatter.14.cloned.1.call-start = ((), (), s32[]{:S(2)}) async-start(), calls=%async_computation.23 | async-start | bytes 7864320 | tf_op jit(solution)/shard_map/reduce_scatter | solution.py:617
  1037.2 322.8 %reduce-scatter.10.cloned.1.call-start = ((), (), s32[]{:S(2)}) async-start(), calls=%async_computation.19 | async-start | bytes 7864320 | tf_op jit(solution)/shard_map/reduce_scatter | solution.py:591
  1067.9 19.4 %all-to-all-start.5 = ((bf16[4,48,3072]{2,1,0:T(8,128)(2,1)}), bf16[4,48,3072]{2,1,0:T(8,128)(2,1)S(1)}, u32[]{:S(2)}, u32[]{:S(2)}) async-start(bf16[4,48,3072]{2,1,0:T(8,128)(2,1)} %bitcast.110), calls=%async_computation.12 | async-start | bytes 2359296 | tf_op jit(solution)/shard_map/all_to_all | solution.py:488
  1087.8 153.9 %copy-start.15 = (f32[48,4096]{1,0:T(8,128)S(1)}, f32[48,4096]{1,0:T(8,128)}, u32[]{:S(2)}) copy-start(f32[48,4096]{1,0:T(8,128)} %param.26) | copy-start | bytes 2359300
  1087.9 155.2 %copy-start.16 = (f32[4,6,8,1024]{3,2,0,1:T(8,128)}, f32[4,6,8,1024]{3,2,0,1:T(8,128)S(1)}, u32[]{:S(2)}) copy-start(f32[4,6,8,1024]{3,2,0,1:T(8,128)S(1)} %copy.127) | copy-start | bytes 2359300
  1135.0 109.0 %copy-start.42 = (f32[48]{0:T(128)S(1)}, f32[48]{0:T(128)}, u32[]{:S(2)}) copy-start(f32[48]{0:T(128)} %param.25) | copy-start | bytes 580
  1135.0 8.2 all-to-all-start.4
  1238.3 13.5 all-to-all-start.3
  1254.2 105.7 %copy-start.27 = (f32[1536]{0:T(1024)S(1)}, f32[1536]{0:T(1024)}, u32[]{:S(2)}) copy-start(f32[1536]{0:T(1024)} %copy-done.26) | copy-start | bytes 18436
  1256.4 109.5 %copy-start.32 = (f32[48,24]{0,1:T(8,128)}, f32[48,24]{0,1:T(8,128)S(1)}, u32[]{:S(2)}) copy-start(f32[48,24]{0,1:T(8,128)S(1)} %reshape.393) | copy-start | bytes 13828
  (41 other events, 1193.1 us)
Sparse Core Ops, SparseCore 0:
  29.0 85.3 all-gather.9
  116.0 44.5 all-gather.7
  183.3 46.0 all-gather.11
  327.6 87.4 reduce-scatter.7
  416.5 46.3 all-gather.17
  465.2 138.0 all-gather.15
  604.9 44.5 all-gather.13
  700.5 58.3 reduce-scatter.11
  765.4 46.3 all-gather.19
  815.2 252.6 reduce-scatter.19
  1071.9 63.0 reduce-scatter.17
  1138.6 99.6 reduce-scatter.15
  1240.8 58.1 reduce-scatter.13
  1301.5 58.3 reduce-scatter.9

commit v2 on v1

--- a/solution.py
+++ b/solution.py
@@ -458,13 +458,241 @@
     )
 
 
-def normalize(hidden):
-    factor = lax.rsqrt(jnp.mean(hidden * hidden, axis=1, keepdims=True) + epsilon)
-    return (hidden * factor, factor)
-
-
-def norm_back(grad_hat, normed, factor):
-    return factor * (grad_hat - normed * jnp.mean(grad_hat * normed, axis=1, keepdims=True))
+PIECES = 4
+
+
+def partners():
+    me = lax.axis_index("head")
+    near = me + 1 - 2 * (me % 2)
+    far = (me + 2) % 4
+    cross = (near + 2) % 4
+    return me, near, far, cross
+
+
+def greet(*others):
+    barrier = pltpu.get_barrier_semaphore()
+    for other in others:
+        pl.semaphore_signal(
+            barrier, inc=1, device_id={"head": other}, device_id_type=pl.DeviceIdType.MESH
+        )
+    pl.semaphore_wait(barrier, len(others))
+
+
+def remote(source, target, send, receive, other):
+    return pltpu.make_async_remote_copy(
+        src_ref=source,
+        dst_ref=target,
+        send_sem=send,
+        recv_sem=receive,
+        device_id={"head": other},
+        device_id_type=pl.DeviceIdType.MESH,
+    )
+
+
+def rows_of(ref, shard, piece, size):
+    span = size // PIECES
+    start = pl.multiple_of(shard * size + piece * span, span)
+    return ref.at[pl.ds(start, span), :]
+
+
+def spread_piece(source_of, all_ref, size, sems, piece):
+    me, near, far, _ = partners()
+    far_send, far_recv, near_send, near_recv, _, _, own = sems
+    copies = (
+        remote(source_of(piece), rows_of(all_ref, me, piece, size), far_send.at[piece], far_recv.at[piece], far),
+        remote(source_of(piece), rows_of(all_ref, me, piece, size), near_send.at[piece], near_recv.at[piece], near),
+        pltpu.make_async_copy(source_of(piece), rows_of(all_ref, me, piece, size), own.at[piece]),
+    )
+    for copy in copies:
+        copy.start()
+    return copies
+
+
+def hand_on(all_ref, size, sems, sent):
+    me, near, far, cross = partners()
+    far_send, far_recv, near_send, near_recv, on_send, on_recv, own = sems
+    passed = []
+    for piece in range(PIECES):
+        there = rows_of(all_ref, far, piece, size)
+        remote(there, there, far_send.at[piece], far_recv.at[piece], far).wait_recv()
+        copy = remote(there, there, on_send.at[piece], on_recv.at[piece], near)
+        copy.start()
+        passed.append(copy)
+    for piece in range(PIECES):
+        to_far, to_near, local = sent[piece]
+        to_far.wait_send()
+        to_near.wait_send()
+        local.wait()
+        passed[piece].wait_send()
+        there = rows_of(all_ref, near, piece, size)
+        remote(there, there, near_send.at[piece], near_recv.at[piece], near).wait_recv()
+        there = rows_of(all_ref, cross, piece, size)
+        remote(there, there, on_send.at[piece], on_recv.at[piece], near).wait_recv()
+
+
+def gather_sems():
+    return [pltpu.SemaphoreType.DMA((PIECES,)) for _ in range(7)]
+
+
+def gather_kernel(mine_ref, all_ref, *sems):
+    size = mine_ref.shape[0]
+    _, near, far, _ = partners()
+    greet(near, far)
+    sent = [
+        spread_piece(lambda n: rows_of(mine_ref, 0, n, size), all_ref, size, sems, piece)
+        for piece in range(PIECES)
+    ]
+    hand_on(all_ref, size, sems, sent)
+
+
+def gather_heads(mine, number):
+    rows, width = mine.shape
+    return pl.pallas_call(
+        gather_kernel,
+        in_specs=[pl.BlockSpec(memory_space=pl.ANY)],
+        out_specs=pl.BlockSpec(memory_space=pl.ANY),
+        out_shape=jax.ShapeDtypeStruct((4 * rows, width), mine.dtype),
+        scratch_shapes=gather_sems(),
+        compiler_params=pltpu.CompilerParams(collective_id=number, has_side_effects=True),
+        cost_estimate=pl.CostEstimate(
+            flops=30_000_000_000, transcendentals=0, bytes_accessed=8_000_000
+        ),
+        name="gather_heads",
+    )(mine)
+
+
+def exchange_kernel(local, extras, gather, *refs):
+    part_ref, rest = refs[0], refs[1:]
+    extra_refs, rest = rest[:extras], rest[extras:]
+    out_ref, rest = rest[0], rest[1:]
+    if gather:
+        all_ref, rest = rest[0], rest[1:]
+    near_buf, turn_buf, far_buf, rest = rest[0], rest[1], rest[2], rest[3:]
+    near_send, near_recv, far_send, far_recv = rest[:4]
+    if gather:
+        payload, sems = rest[4], rest[5:]
+    size = out_ref.shape[0]
+    span = size // PIECES
+    me, near, far, cross = partners()
+    greet(near, far)
+    near_copies = []
+    for which, shard in ((0, cross), (1, near)):
+        for piece in range(PIECES):
+            copy = remote(
+                rows_of(part_ref, shard, piece, size),
+                near_buf.at[which, pl.ds(piece * span, span), :],
+                near_send.at[which, piece],
+                near_recv.at[which, piece],
+                near,
+            )
+            copy.start()
+            near_copies.append(copy)
+    far_copies = []
+    for piece in range(PIECES):
+        here = slice(piece * span, (piece + 1) * span)
+        near_copies[piece].wait_recv()
+        turn_buf[here, :] = (
+            rows_of(part_ref, far, piece, size)[...].astype(f32) + near_buf[0, here, :].astype(f32)
+        ).astype(bf16)
+        copy = remote(
+            turn_buf.at[pl.ds(piece * span, span), :],
+            far_buf.at[pl.ds(piece * span, span), :],
+            far_send.at[piece],
+            far_recv.at[piece],
+            far,
+        )
+        copy.start()
+        far_copies.append(copy)
+    sent = []
+    for piece in range(PIECES):
+        here = slice(piece * span, (piece + 1) * span)
+        near_copies[PIECES + piece].wait_recv()
+        far_copies[piece].wait_recv()
+        total = (
+            rows_of(part_ref, me, piece, size)[...].astype(f32)
+            + near_buf[1, here, :].astype(f32)
+            + far_buf[here, :].astype(f32)
+        )
+        result, share = local(total, here, *extra_refs)
+        out_ref[here, :] = result.astype(out_ref.dtype)
+        if gather:
+            payload[here, :] = share.astype(bf16)
+            sent.append(
+                spread_piece(
+                    lambda n: payload.at[pl.ds(n * span, span), :], all_ref, size, sems, piece
+                )
+            )
+    if gather:
+        hand_on(all_ref, size, sems, sent)
+    for copy in near_copies + far_copies:
+        copy.wait_send()
+
+
+def exchange(local, part, extras, out_type, gather, number, name):
+    rows, width = part.shape
+    size = rows // 4
+    out_shape = [jax.ShapeDtypeStruct((size, width), out_type)]
+    out_specs = [pl.BlockSpec(memory_space=pltpu.VMEM)]
+    scratch = [
+        pltpu.VMEM((2, size, width), bf16),
+        pltpu.VMEM((size, width), bf16),
+        pltpu.VMEM((size, width), bf16),
+        pltpu.SemaphoreType.DMA((2, PIECES)),
+        pltpu.SemaphoreType.DMA((2, PIECES)),
+        pltpu.SemaphoreType.DMA((PIECES,)),
+        pltpu.SemaphoreType.DMA((PIECES,)),
+    ]
+    if gather:
+        out_shape.append(jax.ShapeDtypeStruct((rows, width), bf16))
+        out_specs.append(pl.BlockSpec(memory_space=pl.ANY))
+        scratch += [pltpu.VMEM((size, width), bf16)] + gather_sems()
+    return pl.pallas_call(
+        functools.partial(exchange_kernel, local, len(extras), gather),
+        in_specs=[pl.BlockSpec(memory_space=pltpu.VMEM)] * (1 + len(extras)),
+        out_specs=out_specs,
+        out_shape=out_shape,
+        scratch_shapes=scratch,
+        compiler_params=pltpu.CompilerParams(collective_id=number, has_side_effects=True),
+        cost_estimate=pl.CostEstimate(
+            flops=60_000_000_000 if gather else 35_000_000_000,
+            transcendentals=0,
+            bytes_accessed=16_000_000,
+        ),
+        name=name,
+    )(part, *extras)
+
+
+def inverse_rms(value):
+    return lax.rsqrt(jnp.mean(value * value, axis=1, keepdims=True) + epsilon)
+
+
+def through_norm(grad, value):
+    factor = inverse_rms(value)
+    normed = value * factor
+    return factor * (grad - normed * jnp.mean(grad * normed, axis=1, keepdims=True))
+
+
+def after_attention(total, here, tokens_ref, gain_ref):
+    middle = tokens_ref[here, :].astype(f32) + total
+    return middle, middle * inverse_rms(middle) * gain_ref[0:1, :]
+
+
+def after_hidden(total, here, cotangent_ref, middle_ref, gain_ref):
+    grad = cotangent_ref[here, :].astype(f32) + through_norm(
+        total * gain_ref[0:1, :], middle_ref[here, :]
+    )
+    return grad, grad
+
+
+def after_first(total, here, grad_ref, tokens_ref, gain_ref):
+    grad = grad_ref[here, :] + through_norm(
+        total * gain_ref[0:1, :], tokens_ref[here, :].astype(f32)
+    )
+    return grad, None
+
+
+def after_down(total, here, middle_ref):
+    return middle_ref[here, :] + total, None
 
 
 def over_tokens(operand, other_side):
@@ -473,12 +701,15 @@
     )
 
 
-def gathered(pieces, groups):
+def sent_columns(pieces, groups):
     packed = jnp.concatenate(
         [piece.reshape(piece.shape[0], groups, -1) for piece in pieces], axis=2
     )
     mine = lax.all_to_all(packed, "head", split_axis=1, concat_axis=0, tiled=True)
-    mine = mine.reshape(mine.shape[0], mine.shape[2])
+    return mine.reshape(mine.shape[0], mine.shape[2])
+
+
+def all_rows(mine):
     return lax.all_gather(mine, "blk", axis=0, tiled=True)
 
 
@@ -526,11 +757,16 @@
         [forget_low, spread(norm1_gain), spread(norm2_gain), jnp.zeros((share, groups, rest), bf16)],
         axis=2,
     )
-    first = gathered([low(w_key), low(w_value), low(w_query), low(w_gate_out), small], groups)
-    tokens_all = lax.all_gather(tokens, "head", axis=0, tiled=True)
-    output_weight = gathered([low(w_output)], groups)
-    second = gathered([low(w_gate), low(w_up), low(w_down)], groups)
-    cotangent_all = lax.all_gather(cotangent, "head", axis=0, tiled=True)
+    mine_kv = sent_columns([low(w_key), low(w_value), small], groups)
+    first_kv = all_rows(mine_kv)
+    mine_rest = sent_columns(
+        [low(w_query), low(w_gate_out), low(w_output), low(w_gate), low(w_up), low(w_down)], groups
+    )
+    first_q = all_rows(mine_rest[:, : 3 * local_width])
+    second = all_rows(mine_rest[:, 3 * local_width :])
+    tokens_all = gather_heads(tokens, 0)
+    cotangent_all = gather_heads(cotangent, 1)
+    output_weight = first_q[:, 2 * local_width :]
 
     segment_plus = segment + 1
     earlier_segment = passed_along(segment_plus, "blk", 1)
@@ -542,20 +778,23 @@
     ranges = jnp.stack([tiles[:, 0] // K_TILE, (tiles[:, -1] + K_TILE - 1) // K_TILE])
     begins = jnp.broadcast_to(begins[None, :], (8, rows))
 
-    gain1 = first[:, 4 * local_width + local_heads].astype(f32)
-    gain2 = first[:, 4 * local_width + local_heads + 1].astype(f32)
-    normed_all, _ = normalize(tokens_all.astype(f32))
-    input1 = (normed_all * gain1).astype(bf16)
-    key_value = dot(input1, first[:, : 2 * local_width]).astype(bf16)
+    def gain_rows(column):
+        gain = first_kv[:, 2 * local_width + local_heads + column].astype(f32)
+        return jnp.broadcast_to(gain[None, :], (8, model_width))
+
+    gain1, gain2 = gain_rows(0), gain_rows(1)
+    wide_all = tokens_all.astype(f32)
+    input1 = (wide_all * inverse_rms(wide_all) * gain1[0:1]).astype(bf16)
+    key_value = dot(input1, first_kv[:, : 2 * local_width]).astype(bf16)
     earlier_kv = passed_along(key_value, "blk", 1)
-    query = dot(input1, first[:, 2 * local_width : 3 * local_width]).astype(bf16)
-    gate_forget = dot(input1, first[:, 3 * local_width :])
-    gate_raw = gate_forget[:, :local_width]
     bias = lax.dynamic_slice_in_dim(forget_bias, group * local_heads, local_heads, 0)
     bias = jnp.pad(bias, (0, LANES - local_heads))
-    forget = (gate_forget[:, local_width:] + bias[None, :]).astype(bf16).astype(f32)
+    forget = dot(input1, first_kv[:, 2 * local_width :]) + bias[None, :]
+    forget = forget.astype(bf16).astype(f32)
     terms, halo_terms = decay_terms(jax.nn.log_sigmoid(forget), local_heads)
     earlier_terms = passed_along(halo_terms, "blk", 1)
+    query = dot(input1, first_q[:, :local_width]).astype(bf16)
+    gate_raw = dot(input1, first_q[:, local_width : 2 * local_width])
 
     attended, lse = attend(
         ranges, query, key_value, earlier_kv, terms, earlier_terms, begins, local_heads
@@ -564,11 +803,8 @@
     attended_wide = attended.astype(f32)
     gated = (opened * attended_wide).astype(bf16)
     branch = dot(gated, output_weight, NT).astype(bf16)
-    inputs = tokens.astype(f32)
-    middle = inputs + lax.psum_scatter(branch, "head", scatter_dimension=0, tiled=True).astype(f32)
-    normed2, factor2 = normalize(middle)
-    input2 = lax.all_gather(
-        (normed2 * gain2).astype(bf16), "head", axis=0, tiled=True
+    middle, input2 = exchange(
+        after_attention, branch, [tokens, gain2], f32, True, 2, "exchange_middle"
     )
     gate_act = dot(input2, second[:, :hidden_width])
     up_act = dot(input2, second[:, hidden_width : 2 * hidden_width])
@@ -582,14 +818,9 @@
     grad_up_act = (grad_hidden * gate_act * opening).astype(bf16)
     grad_act = jnp.concatenate([grad_gate_act, grad_up_act], axis=1)
     grad_input2 = dot(grad_act, second[:, : 2 * hidden_width], NT).astype(bf16)
-    grad_input2 = lax.psum_scatter(
-        grad_input2, "head", scatter_dimension=0, tiled=True
-    ).astype(f32)
-    grad_middle = cotangent.astype(f32) + norm_back(grad_input2 * gain2, normed2, factor2)
-    grad_branch = lax.all_gather(grad_middle.astype(bf16), "head", axis=0, tiled=True)
-    result = (
-        middle + lax.psum_scatter(down, "head", scatter_dimension=0, tiled=True).astype(f32)
-    ).astype(bf16)
+    grad_middle, grad_branch = exchange(
+        after_hidden, grad_input2, [cotangent, middle, gain2], f32, True, 3, "exchange_hidden"
+    )
     second_grad = jnp.concatenate(
         [over_tokens(input2, grad_act).astype(bf16), over_tokens(cotangent_all, hidden).astype(bf16)],
         axis=1,
@@ -599,7 +830,11 @@
     grad_gated = dot(grad_branch, output_weight)
     grad_attended = (grad_gated * opened).astype(bf16)
     grad_gate_pre = (grad_gated * attended_wide * opened * (1.0 - opened)).astype(bf16)
-    output_sum = scattered(over_tokens(grad_branch, gated).astype(bf16), groups)
+    early_grad = jnp.concatenate(
+        [over_tokens(input1, grad_gate_pre).astype(bf16), over_tokens(grad_branch, gated).astype(bf16)],
+        axis=1,
+    )
+    early_sum = scattered(early_grad, groups)
 
     dq, dk_own, dv_own, dk_prev, dv_prev, decay_own, decay_prev = attend_back(
         ranges, query, key_value, earlier_kv, terms, earlier_terms, begins,
@@ -612,39 +847,43 @@
     forget_grad = jnp.where(
         jnp.arange(LANES)[None, :] < local_heads, logf_grad * jax.nn.sigmoid(-forget), 0.0
     ).astype(bf16)
-    grads = jnp.concatenate([dk, dv, dq, grad_gate_pre, forget_grad], axis=1)
-    grad_input1 = dot(grads, first, NT).astype(bf16)
-    grad_input1 = lax.psum_scatter(
-        grad_input1, "head", scatter_dimension=0, tiled=True
-    ).astype(f32)
-    normed1, factor1 = normalize(inputs)
-    tokens_grad = grad_middle + norm_back(grad_input1 * gain1, normed1, factor1)
-
+    grads = jnp.concatenate([dk, dv, forget_grad, dq], axis=1)
     first_grad = over_tokens(input1, grads)
     bias_part = jnp.sum(forget_grad.astype(f32), axis=0)
     row = jnp.arange(model_width)[:, None] % share
-    column = jnp.arange(4 * local_width + LANES)[None, :]
+    column = jnp.arange(3 * local_width + LANES)[None, :]
     spread_bias = jnp.sum(
-        jnp.where(row[:, :, None] == jnp.arange(local_heads)[None, None, :], bias_part[:local_heads], 0.0),
-        axis=2,
+        jnp.where(row == jnp.arange(LANES)[None, :], bias_part[None, :], 0.0), axis=1, keepdims=True
     )
     first_grad = jnp.where(
-        column == 4 * local_width + local_heads, spread_bias, first_grad
+        column == 2 * local_width + local_heads, spread_bias, first_grad
     ).astype(bf16)
     first_sum = scattered(first_grad, groups)
+    kv_width = 2 * local_width + LANES
+    grad_input1 = (
+        dot(grads[:, :kv_width], first_kv, NT)
+        + dot(
+            jnp.concatenate([dq, grad_gate_pre], axis=1), first_q[:, : 2 * local_width], NT
+        )
+    ).astype(bf16)
+    (tokens_grad,) = exchange(
+        after_first, grad_input1, [grad_middle, tokens, gain1], f32, False, 4, "exchange_first"
+    )
+    (result,) = exchange(after_down, down, [middle], bf16, False, 5, "exchange_down")
 
     def columns(array, start, width):
         return array[:, :, start : start + width].reshape(share, groups * width)
 
-    key_sum, value_sum, query_sum, gate_out_sum = (
-        columns(first_sum, n * local_width, local_width) for n in range(4)
-    )
-    forget_sum = columns(first_sum, 4 * local_width, local_heads)
-    bias_total = first_sum[:local_heads, :, 4 * local_width + local_heads].T.reshape(head_count)
+    key_sum, value_sum = (columns(first_sum, n * local_width, local_width) for n in range(2))
+    forget_sum = columns(first_sum, 2 * local_width, local_heads)
+    bias_total = first_sum[:local_heads, :, 2 * local_width + local_heads].T.reshape(head_count)
+    query_sum = columns(first_sum, kv_width, local_width)
+    gate_out_sum, output_total = (
+        columns(early_sum, n * local_width, local_width) for n in range(2)
+    )
     gate_sum, up_sum, down_sum = (
         columns(second_sum, n * hidden_width, hidden_width) for n in range(3)
     )
-    output_total = columns(output_sum, 0, local_width)
 
     def along(weight, grad):
         return jnp.sum(low(weight).astype(f32) * grad, axis=1)

time: 1380 us -> 1170 us (0.85)
  waiting for transfers between devices: 899 us -> 382 us
  Pallas kernels: 135 us -> 467 us
  other arithmetic: 57.7 us -> 36.2 us
    all_gather x7 -> x3, waiting for transfers between devices: 354 us -> 0.06 us  [all_rows(): return lax.all_gather(mine, 'blk', axis=0, tiled=True)]
    pallas_call x0 -> x6, Pallas kernels: none -> 347 us  [the longest x4 247 us: exchange(): pl.pallas_call(functools.partial(exchange_kernel, local, len(extras), gat...]
    reduce_scatter x4 -> x0, waiting for transfers between devices: 216 us -> none  [the longest x1 65.1 us: body(): lax.psum_scatter(branch, 'head', scatter_dimension=0, tiled=True)]
    ppermute x6, waiting for transfers between devices: 140 us -> 237 us  [passed_along(): return lax.ppermute(array, axis, pairs)]
    reduce_scatter x3, waiting for transfers between devices: 160 us -> 126 us  [scattered(): summed = lax.psum_scatter(grad, 'blk', scatter_dimension=0, tiled=True)]
    dot_general x11 -> x13, matrix products: 131 us -> 141 us  [dot(): return lax.dot_general(a, b, dims, preferred_element_type=f32, **kw)]
    dot_general x4 -> x5, matrix products: 50.2 us -> 46.9 us  [over_tokens(): lax.dot_general(operand, other_side, (((0,), (0,)), ((), ())), preferred_...]
  transfers between devices with their start and end apart: 24 -> 15, of which waited for: 20 -> 6; matrix products, arithmetic and copies ran while one was open for 13% -> 13% of each run, Pallas kernels for 10% -> 33%
where the time goes in v2:
time: 1170 us
  Pallas kernels  467 us (40%)
  waiting for transfers between devices  382 us (33%)
  matrix products  188 us (16%)
  other arithmetic  36.2 us (3%)
  blocking collectives  34.2 us (3%)
  starting transfers between devices  25.6 us (2%)
  local copies, waits for them, and re-layouts  20.6 us (2%)
  between operations  15.4 us (1%)
    pallas_call x4, Pallas kernels, exchange(): pl.pallas_call(functools.partial(exchange_kernel, local, len(extras), gat...  247 us
    ppermute x6, waiting for transfers between devices, passed_along(): return lax.ppermute(array, axis, pairs)  237 us
    dot_general x13, matrix products, dot(): return lax.dot_general(a, b, dims, preferred_element_type=f32, **kw)  141 us
    reduce_scatter x3, waiting for transfers between devices, scattered(): summed = lax.psum_scatter(grad, 'blk', scatter_dimension=0, tiled=True)  126 us
    pallas_call x2, Pallas kernels, gather_heads(): pl.pallas_call(gather_kernel, in_specs=[pl.BlockSpec(memory_space=pl.ANY)...  100 us
    pallas_call x1, Pallas kernels, attend_back(): pl.pallas_call(functools.partial(attend_back_kernel, local_heads), grid_s...  64.6 us
    dot_general x5, matrix products, over_tokens(): lax.dot_general(operand, other_side, (((0,), (0,)), ((), ())), preferred_...  46.9 us
    pallas_call x1, Pallas kernels, attend(): pl.pallas_call(functools.partial(attend_kernel, local_heads), grid_spec=p...  46.5 us
  transfers between devices with their start and end apart: 15, of which 6 were waited for; matrix products, arithmetic and copies ran while one was open for 13% of the time, Pallas kernels for 33%

profile of v2, /device:TPU:0, one launch (start us, length us, event | category | flops | bytes accessed | tf_op | source)
XLA Modules:
  0.0 1167.9 jit_solution(8735862980093414474)
XLA Ops:
  12.6 11.2 all_to_all.45
  27.6 23.0 %all_to_all.46 = bf16[48,4,4224]{2,0,1:T(8,128)(2,1)S(1)} all-to-all(bf16[48,4,4224]{2,0,1:T(8,128)(2,1)S(1)} %copy.114), channel_id=1, replica_groups=mesh['blk'=8,'head'=4] {'head'}, dimensions={1} | all-to-all | bytes 3244032 | tf_op jit(solution)/shard_map/all_to_all | solution.py:708
  55.3 49.4 %gather_heads.2 = bf16[2048,1536]{1,0:T(8,128)(2,1)} custom-call(bf16[512,1536]{1,0:T(8,128)(2,1)} %refs_2_.1), custom_call_target="tpu_custom_call" | custom-call | flops 30000001024 | bytes 8000000 | tf_op jit(solution)/shard_map/gather_heads/pallas_call | solution.py:550
  104.7 50.7 %gather_heads.3 = bf16[2048,1536]{1,0:T(8,128)(2,1)} custom-call(bf16[512,1536]{1,0:T(8,128)(2,1)} %refs_1_.3), custom_call_target="tpu_custom_call" | custom-call | flops 30000001024 | bytes 8000000 | tf_op jit(solution)/shard_map/gather_heads/pallas_call | solution.py:550
  167.8 6.4 convolution_convert_fusion.5.k_own_ref.v_own_ref
  183.6 6.1 fusion.44
  195.2 8.5 add_divide_fusion.1
  203.7 7.7 convolution_convert_fusion.8.q_ref
  211.4 65.8 %collective-permute-done.2.t_prev_ref = bf16[2048,128]{1,0:T(8,128)(2,1)S(1)} collective-permute-done((bf16[2048,128]{1,0:T(8,128)(2,1)}, bf16[2048,128]{1,0:T(8,128)(2,1)S(1)}, u32[]{:S(2)}, u32[]{:S(2)}) %collective-permute-start.2) | collective-permute-done | bytes 524320 | tf_op jit(solution)/shard_map/ppermute | solution.py:28
  278.0 46.5 %attend.1 = (bf16[2048,384]{1,0:T(8,128)(2,1)}, f32[24,2048]{1,0:T(8,128)}) custom-call(s32[2,4]{1,0:T(2,128)} %pad_add_fusion.1.ranges_ref, bf16[2048,384]{1,0:T(8,128)(2,1)} %convolution_convert_fusion.8.q_ref, bf16[2048,768]{1,0:T(8,128)(2,1)} %convolution_convert_fusion.5.k_own_ref.v_own_ref, ...), custom_call_target="tpu_custom_call" | custom-call | flops 40000000000 | bytes 12000000 | tf_op jit(solution)/shard_map/attend/pallas_call | solution.py:249
  324.5 8.8 convolution_convert_fusion.1.refs_0_
  333.9 78.5 %exchange_middle.1 = (f32[512,1536]{1,0:T(8,128)}, bf16[2048,1536]{1,0:T(8,128)(2,1)}) custom-call(bf16[2048,1536]{1,0:T(8,128)(2,1)} %convolution_convert_fusion.1.refs_0_, bf16[512,1536]{1,0:T(8,128)(2,1)} %refs_2_.1, f32[8,1536]{1,0:T(8,128)} %broadcast_in_dim.48.refs_2_.refs_3_), custom_call_target="tpu_custom_call" | custom-call | flops 60000002048 | bytes 16000000 | tf_op jit(solution)/shard_map/exchange_middle/pallas_call | solution.py:649
  412.5 11.9 %fusion.30 = f32[2048,1024]{0,1:T(8,128)} fusion(bf16[2048,1536]{1,0:T(8,128)(2,1)} %get-tuple-element.32, bf16[1536,3072]{1,0:T(8,128)(2,1)} %all-gather.8.cloned.1.call-done), kind=kOutput, calls=%fused_computation.49 | convolution fusion | flops 6442450944 | bytes 17825792 | tf_op jit(solution)/shard_map/dot_general | solution.py:22
  424.4 12.3 %fusion.35 = f32[1024,2048]{1,0:T(8,128)} fusion(bf16[2048,1536]{1,0:T(8,128)(2,1)} %gather_heads.3, bf16[1536,3072]{1,0:T(8,128)(2,1)} %all-gather.8.cloned.1.call-done), kind=kOutput, calls=%fused_computation.62 | convolution fusion | flops 6442450944 | bytes 17825792 | tf_op jit(solution)/shard_map/dot_general | solution.py:22
  436.6 19.7 %fusion.5 = (bf16[2048,1024]{0,1:T(8,128)(2,1)}, bf16[2048,1024]{0,1:T(8,128)(2,1)}, bf16[2048,1024]{0,1:T(8,128)(2,1)}) fusion(f32[1024,2048]{1,0:T(8,128)} %fusion.35, f32[2048,1024]{0,1:T(8,128)} %fusion.30, bf16[2048,1536]{1,0:T(8,128)(2,1)} %get-tuple-element.32, bf16[1536,3072]{1,0:T(8,128)(2,1)} %all-gather.8.cloned.1.call-done), kind=kOutput, calls=%fused_computation.14 | convolution fusion | flops 6476005376 | bytes 38797312 | tf_op jit(solution)/shard_map/dot_general | solution.py:22
  456.3 19.3 %convolution_convert_fusion.3.refs_0_ = bf16[2048,1536]{1,0:T(8,128)(2,1)} fusion(bf16[1536,3072]{1,0:T(8,128)(2,1)} %all-gather.8.cloned.1.call-done, bf16[2048,1024]{0,1:T(8,128)(2,1)} %get-tuple-element.51, bf16[2048,1024]{0,1:T(8,128)(2,1)} %get-tuple-element.50), kind=kOutput, calls=%fused_computation.23 | convolution fusion | flops 12904824832 | bytes 20971520 | tf_op jit(solution)/shard_map/dot_general | solution.py:22
  475.6 80.3 %exchange_hidden.1 = (f32[512,1536]{1,0:T(8,128)}, bf16[2048,1536]{1,0:T(8,128)(2,1)}) custom-call(bf16[2048,1536]{1,0:T(8,128)(2,1)} %convolution_convert_fusion.3.refs_0_, bf16[512,1536]{1,0:T(8,128)(2,1)} %refs_1_.3, f32[512,1536]{1,0:T(8,128)} %get-tuple-element.33.refs_1_.refs_2_, f32[8,1536]{1,0:T(8,128)} %broadcast_in_dim.48.refs_2_.refs_3_), custom_call_target="tpu_custom_call" | custom-call | flops 60000002048 | bytes 16000000 | tf_op jit(solution)/shard_map/exchange_hidden/pallas_call | solution.py:649
  562.1 6.6 fusion.27
  574.1 64.6 %attend_back.1 = (bf16[2048,384]{1,0:T(8,128)(2,1)}, f32[2048,384]{1,0:T(8,128)}, f32[2048,384]{1,0:T(8,128)}, bf16[2048,384]{1,0:T(8,128)(2,1)}, bf16[2048,384]...) custom-call(s32[2,4]{1,0:T(2,128)} %pad_add_fusion.1.ranges_ref, ...), custom_call_target="tpu_custom_call" | custom-call | flops 80000000000 | bytes 25000000 | tf_op jit(solution)/shard_map/attend_back/pallas_call | solution.py:410
  642.7 148.4 %collective-permute-done.5.halo_ref = f32[2048,128]{1,0:T(8,128)S(1)} collective-permute-done((f32[2048,128]{1,0:T(8,128)}, f32[2048,128]{1,0:T(8,128)S(1)}, u32[]{:S(2)}, u32[]{:S(2)}) %collective-permute-start.5) | collective-permute-done | bytes 1048608 | tf_op jit(solution)/shard_map/ppermute | solution.py:28
  801.6 23.0 %collective-permute-done.4 = bf16[2048,384]{1,0:T(8,128)(2,1)} collective-permute-done((bf16[2048,384]{1,0:T(8,128)(2,1)}, bf16[2048,384]{1,0:T(8,128)(2,1)}, u32[]{:S(2)}, u32[]{:S(2)}) %collective-permute-start.4) | collective-permute-done | bytes 1572896 | tf_op jit(solution)/shard_map/ppermute | solution.py:28
  827.5 11.2 fusion.8
  838.8 10.4 fusion.23
  849.3 16.6 %convolution_convert_fusion.2 = bf16[1536,2048]{1,0:T(8,128)(2,1)S(1)} fusion(bf16[2048,1536]{1,0:T(8,128)(2,1)} %get-tuple-element.32, bf16[2048,1024]{0,1:T(8,128)(2,1)} %get-tuple-element.51, bf16[2048,1024]{0,1:T(8,128)(2,1)S(1)} %copy-done.45), kind=kOutput, calls=%fused_computation.22 | convolution fusion | flops 12904824832 | bytes 20971520 | tf_op jit(solution)/shard_map/dot_general | solution.py:699
  870.5 11.8 %convolution_convert_fusion.refs_0_ = bf16[2048,1536]{1,0:T(8,128)(2,1)} fusion(bf16[2048,1024]{0,1:T(8,128)(2,1)} %get-tuple-element.52, bf16[1536,3072]{1,0:T(8,128)(2,1)} %all-gather.8.cloned.1.call-done), kind=kOutput, calls=%fused_computation.20 | convolution fusion | flops 6445596672 | bytes 13631488 | tf_op jit(solution)/shard_map/dot_general | solution.py:22
  882.3 43.3 %exchange_down.1 = bf16[512,1536]{1,0:T(8,128)(2,1)} custom-call(bf16[2048,1536]{1,0:T(8,128)(2,1)} %convolution_convert_fusion.refs_0_, f32[512,1536]{1,0:T(8,128)} %get-tuple-element.33.refs_1_.refs_2_), custom_call_target="tpu_custom_call" | custom-call | flops 35000000512 | bytes 16000000 | tf_op jit(solution)/shard_map/exchange_down/pallas_call | solution.py:649
  925.6 11.6 fusion.17
  937.3 10.1 add_convert_fusion.refs_0_
  951.5 45.1 %exchange_first.1 = f32[512,1536]{1,0:T(8,128)} custom-call(bf16[2048,1536]{1,0:T(8,128)(2,1)} %add_convert_fusion.refs_0_, f32[512,1536]{1,0:T(8,128)} %get-tuple-element.43.refs_1_, bf16[512,1536]{1,0:T(8,128)(2,1)} %refs_2_.1, f32[8,1536]{1,0:T(8,128)} %broadcast_in_dim.50.refs_3_), custom_call_target="tpu_custom_call" | custom-call | flops 35000000512 | bytes 16000000 | tf_op jit(solution)/shard_map/exchange_first/pallas_call | solution.py:649
  1001.2 7.4 all-to-all-done.2
  1008.7 126.4 %reduce-scatter.8.cloned.1.call-done = bf16[192,3072]{1,0:T(8,128)(2,1)} async-done(((bf16[1536,3072]{1,0:T(8,128)(2,1)}), bf16[192,3072]{1,0:T(8,128)(2,1)}) %reduce-scatter.8.cloned.1.call-update) | async-done | bytes 1179664 | tf_op jit(solution)/shard_map/reduce_scatter | solution.py:717
  1144.2 10.5 all-to-all-done.4
  (227 shorter events, 99.5 us)
Async XLA Ops:
  7.2 18.5 %copy-start.5 = (f32[48,4096]{1,0:T(8,128)S(1)}, f32[48,4096]{1,0:T(8,128)}, u32[]{:S(2)}) copy-start(f32[48,4096]{1,0:T(8,128)} %param.26) | copy-start | bytes 2359300
  7.2 153.7 %all-gather.4.cloned.1.call-start = ((), (), s32[]{:S(2)}) async-start(), calls=%async_computation.8 | async-start | bytes 3096576 | tf_op jit(solution)/shard_map/all_gather | solution.py:713
  23.8 171.5 %all-gather.6.cloned.1.call-start = ((), (), s32[]{:S(2)}) async-start(), calls=%async_computation.9 | async-start | bytes 3981312 | tf_op jit(solution)/shard_map/all_gather | solution.py:713
  27.4 24.1 %copy-start.32 = (s32[2048]{0:T(1024)S(1)}, s32[2048]{0:T(1024)}, u32[]{:S(2)}) copy-start(s32[2048]{0:T(1024)} %param.16) | copy-start | bytes 24580
  51.5 361.0 %all-gather.8.cloned.1.call-start = ((), (), s32[]{:S(2)}) async-start(), calls=%async_computation.10 | async-start | bytes 10616832 | tf_op jit(solution)/shard_map/all_gather | solution.py:713
  51.5 109.4 %collective-permute-start = (s32[2048]{0:T(1024)S(1)}, s32[2048]{0:T(1024)S(1)}, u32[]{:S(2)}, u32[]{:S(2)}) collective-permute-start(s32[2048]{0:T(1024)S(1)} %broadcast_add_fusion), channel_id=1, source_target_pairs={{0,4},{4,8},{8,12},{12,16},{16,20},{20,24},{24,28},{1,5},{5,9},{9,... | collective-permute-start | bytes 24584 | tf_op jit(solution)/shard_map/ppermute | solution.py:28
  156.6 790.8 %reduce-scatter.10.cloned.1.call-start = ((), (), s32[]{:S(2)}) async-start(), calls=%async_computation.13 | async-start | bytes 2654208 | tf_op jit(solution)/shard_map/reduce_scatter | solution.py:717
  174.2 103.0 %collective-permute-start.1 = (bf16[2048,768]{1,0:T(8,128)(2,1)}, bf16[2048,768]{1,0:T(8,128)(2,1)}, u32[]{:S(2)}, u32[]{:S(2)}) collective-permute-start(bf16[2048,768]{1,0:T(8,128)(2,1)} %convolution_convert_fusion.5.k_own_ref.v_own_ref), channel_id=1, source_target_pairs={{0,4},{4,8},{8,12},{12,16},{16,20},{20,24},{24,28},{1,5},{5,9},{9,... | collective-permute-start | bytes 9437192 | tf_op jit(solution)/shard_map/ppermute | solution.py:28
  193.4 83.8 %collective-permute-start.2 = (bf16[2048,128]{1,0:T(8,128)(2,1)}, bf16[2048,128]{1,0:T(8,128)(2,1)S(1)}, u32[]{:S(2)}, u32[]{:S(2)}) collective-permute-start(bf16[2048,128]{1,0:T(8,128)(2,1)} %get-tuple-element.30), channel_id=1, source_target_pairs={{0,4},{4,8},{8,12},{12,16},{16,20},{20,24},{24,28},{1,5},{5,9},{9,... | collective-permute-start | bytes 1572872 | tf_op jit(solution)/shard_map/ppermute | solution.py:28
  475.6 80.3 %copy-start.38 = (f32[2048,384]{1,0:T(8,128)S(1)}, f32[2048,384]{1,0:T(8,128)}, u32[]{:S(2)}) copy-start(f32[2048,384]{1,0:T(8,128)} %add_divide_fusion.1) | copy-start | bytes 9437188
  574.1 422.6 %reduce-scatter.6.cloned.1.call-start = ((), (), s32[]{:S(2)}) async-start(), calls=%async_computation.11 | async-start | bytes 4423680 | tf_op jit(solution)/shard_map/reduce_scatter | solution.py:717
  574.1 222.4 %copy-start.22 = (f32[2048,128]{1,0:T(8,128)S(1)}, f32[2048,128]{1,0:T(8,128)}, u32[]{:S(2)}) copy-start(f32[2048,128]{1,0:T(8,128)} %get-tuple-element.64) | copy-start | bytes 3145732
  638.7 160.0 %collective-permute-start.3 = (bf16[2048,384]{1,0:T(8,128)(2,1)}, bf16[2048,384]{1,0:T(8,128)(2,1)}, u32[]{:S(2)}, u32[]{:S(2)}) collective-permute-start(bf16[2048,384]{1,0:T(8,128)(2,1)} %get-tuple-element.37), channel_id=1, source_target_pairs={{4,0},{8,4},{12,8},{16,12},{20,16},{24,20},{28,24},{5,1},{9,5},{13... | collective-permute-start | bytes 4718600 | tf_op jit(solution)/shard_map/ppermute | solution.py:28
  640.0 151.0 %collective-permute-start.5 = (f32[2048,128]{1,0:T(8,128)}, f32[2048,128]{1,0:T(8,128)S(1)}, u32[]{:S(2)}, u32[]{:S(2)}) collective-permute-start(f32[2048,128]{1,0:T(8,128)} %get-tuple-element.41), channel_id=1, source_target_pairs={{4,0},{8,4},{12,8},{16,12},{20,16},{24,20},{28,24},{5,1},{9,5},{13... | collective-permute-start | bytes 3145736 | tf_op jit(solution)/shard_map/ppermute | solution.py:28
  641.3 183.2 %collective-permute-start.4 = (bf16[2048,384]{1,0:T(8,128)(2,1)}, bf16[2048,384]{1,0:T(8,128)(2,1)}, u32[]{:S(2)}, u32[]{:S(2)}) collective-permute-start(bf16[2048,384]{1,0:T(8,128)(2,1)} %get-tuple-element.39), channel_id=1, source_target_pairs={{4,0},{8,4},{12,8},{16,12},{20,16},{24,20},{28,24},{5,1},{9,5},{13... | collective-permute-start | bytes 4718600 | tf_op jit(solution)/shard_map/ppermute | solution.py:28
  792.0 35.5 %slice-start.2 = ((s8[6291456]{0:T(1024)(128)(4,1)}), s8[2097152]{0:T(1024)(128)(4,1)S(1)}, s32[]{:S(2)}) async-start(s8[6291456]{0:T(1024)(128)(4,1)} %bitcast.101), calls=%async_computation.16 | async-start | bytes 4194304
  796.5 28.0 %copy-start.2 = (f32[2048,384]{1,0:T(8,128)S(1)}, f32[2048,384]{1,0:T(8,128)}, u32[]{:S(2)}) copy-start(f32[2048,384]{1,0:T(8,128)} %get-tuple-element.38) | copy-start | bytes 9437188
  798.2 28.2 %copy-start.26 = (bf16[2048,128]{1,0:T(8,128)(2,1)}, bf16[2048,128]{1,0:T(8,128)(2,1)S(1)}, u32[]{:S(2)}) copy-start(bf16[2048,128]{1,0:T(8,128)(2,1)S(1)} %get-tuple-element.49) | copy-start | bytes 1572868
  798.7 28.8 %slice-start.3 = ((s8[6291456]{0:T(1024)(128)(4,1)}), s8[4194304]{0:T(1024)(128)(4,1)S(1)}, s32[]{:S(2)}) async-start(s8[6291456]{0:T(1024)(128)(4,1)} %bitcast.101), calls=%async_computation.17 | async-start | bytes 8388608
  801.6 24.9 %copy-start.10 = (bf16[2048,384]{1,0:T(8,128)(2,1)}, bf16[2048,384]{1,0:T(8,128)(2,1)S(1)}, u32[]{:S(2)}) copy-start(bf16[2048,384]{1,0:T(8,128)(2,1)S(1)} %add_convert_fusion.2) | copy-start | bytes 4718596
  801.6 26.0 %copy-start.43 = (bf16[2048,384]{1,0:T(8,128)(2,1)S(1)}, bf16[2048,384]{1,0:T(8,128)(2,1)}, u32[]{:S(2)}) copy-start(bf16[2048,384]{1,0:T(8,128)(2,1)} %get-tuple-element.42) | copy-start | bytes 4718596
  838.7 296.4 %reduce-scatter.8.cloned.1.call-start = ((), (), s32[]{:S(2)}) async-start(), calls=%async_computation.12 | async-start | bytes 10616832 | tf_op jit(solution)/shard_map/reduce_scatter | solution.py:717
  882.3 43.3 %copy-start.11 = (bf16[2048,384]{1,0:T(8,128)(2,1)S(1)}, bf16[2048,384]{1,0:T(8,128)(2,1)}, u32[]{:S(2)}) copy-start(bf16[2048,384]{1,0:T(8,128)(2,1)} %copy-done.10) | copy-start | bytes 4718596
  882.3 43.3 %copy-start.13 = (bf16[2048,384]{1,0:T(8,128)(2,1)S(1)}, bf16[2048,384]{1,0:T(8,128)(2,1)}, u32[]{:S(2)}) copy-start(bf16[2048,384]{1,0:T(8,128)(2,1)} %copy-done.12) | copy-start | bytes 4718596
  947.4 49.2 %all-to-all-start.3 = ((bf16[4,48,768]{2,1,0:T(8,128)(2,1)}), bf16[4,48,768]{2,1,0:T(8,128)(2,1)S(1)}, u32[]{:S(2)}, u32[]{:S(2)}) async-start(bf16[4,48,768]{2,1,0:T(8,128)(2,1)} %bitcast.119), calls=%async_computation.4 | async-start | bytes 589824 | tf_op jit(solution)/shard_map/all_to_all | solution.py:719
  996.7 12.0 %all-to-all-start.2 = ((bf16[4,48,1280]{2,1,0:T(8,128)(2,1)}), bf16[4,48,1280]{2,1,0:T(8,128)(2,1)S(1)}, u32[]{:S(2)}, u32[]{:S(2)}) async-start(bf16[4,48,1280]{2,1,0:T(8,128)(2,1)} %bitcast.118), calls=%async_computation.3 | async-start | bytes 983040 | tf_op jit(solution)/shard_map/all_to_all | solution.py:719
  1000.2 140.1 %copy-start.20 = (f32[4,6,8,384]{3,2,0,1:T(8,128)}, f32[4,6,8,384]{3,2,0,1:T(8,128)S(1)}, u32[]{:S(2)}) copy-start(f32[4,6,8,384]{3,2,0,1:T(8,128)S(1)} %copy.139) | copy-start | bytes 884740
  1001.2 140.1 %copy-start.31 = (f32[48,24]{0,1:T(8,128)S(1)}, f32[48,24]{0,1:T(8,128)}, u32[]{:S(2)}) copy-start(f32[48,24]{0,1:T(8,128)} %param.22) | copy-start | bytes 13828
  1001.2 140.1 %copy-start.16 = (f32[48,1536]{1,0:T(8,128)S(1)}, f32[48,1536]{1,0:T(8,128)}, u32[]{:S(2)}) copy-start(f32[48,1536]{1,0:T(8,128)} %param.20) | copy-start | bytes 884740
  1001.2 141.2 %copy-start.17 = (f32[48,1536]{1,0:T(8,128)S(1)}, f32[48,1536]{1,0:T(8,128)}, u32[]{:S(2)}) copy-start(f32[48,1536]{1,0:T(8,128)} %param.19) | copy-start | bytes 884740
  1008.7 134.8 %copy-start.19 = (f32[48,1536]{1,0:T(8,128)S(1)}, f32[48,1536]{1,0:T(8,128)}, u32[]{:S(2)}) copy-start(f32[48,1536]{1,0:T(8,128)} %param.18) | copy-start | bytes 884740
  1135.1 19.5 %all-to-all-start.4 = ((bf16[4,48,3072]{2,1,0:T(8,128)(2,1)}), bf16[4,48,3072]{2,1,0:T(8,128)(2,1)S(1)}, u32[]{:S(2)}, u32[]{:S(2)}) async-start(bf16[4,48,3072]{2,1,0:T(8,128)(2,1)} %bitcast.108), calls=%async_computation.6 | async-start | bytes 2359296 | tf_op jit(solution)/shard_map/all_to_all | solution.py:719
  (33 other events, 244.2 us)
Sparse Core Ops, SparseCore 0:
  23.9 56.8 all-gather.3
  83.6 63.7 all-gather.5
  156.8 200.2 all-gather.7
  574.2 176.8 reduce-scatter.9
  838.9 129.3 reduce-scatter.5
  972.1 162.9 reduce-scatter.7
